TPU v7x, 128 devices: a whole 4x4x4 slice. The times are simulated.
128 devices in a mesh: own: 4 (over x), seq: 8 (over z, y_hi), tp: 4 (over y_lo, core).
Axes of the slice: x: 4, y: 4 (y_hi: 2, y_lo: 2; y = y_hi * 2 + y_lo), z: 4, core: 2. Of those that a mesh axis runs over, the one named last changes fastest.
Arguments:
- latents: bfloat16 [1, 8192, 5120], P(None, ('own', 'seq')), may hold values from -6 to 6
- policy_out: bfloat16 [1, 8192, 5120], P(None, ('own', 'seq'), 'tp'), may hold values from -6 to 6
- w_qkv: bfloat16 [16, 5120, 3, 2560], P('own', 'seq', None, 'tp'), may hold values from -0.078125 to 0.078125
- w_out: bfloat16 [16, 2560, 5120], P('own', 'tp', 'seq'), may hold values from -0.125 to 0.125
- qk_gains: bfloat16 [16, 2, 2560], P('own', None, 'tp'), may hold values from 2 to 8
- mod_table: float32 [8, 3, 5120], replicated, may hold values from -3 to 3
- timestep: int32 [1], replicated, may hold values from 0 to 7
- owner: int32 [1], replicated, may hold values from 0 to 15
Outputs:
- block_out: bfloat16 [1, 8192, 5120], P(None, ('own', 'seq'), 'tp')
- sq_err: float32 [1, 8192], P(None, ('own', 'seq'))
All inputs are finite; a program needn't handle non-finite values.
Results may differ from a plain program's by a relative error of at most 0.0069.
Values may be sent and summed in bfloat16 or wider, within the bound.
A program may use at most 192 MiB of HBM per device.

v0:
```python
import jax
import jax.numpy as jnp
from jax import lax
from jax.sharding import PartitionSpec as P

D = 5120
HD = 128
HW = 2560


def spread_2(value, axis, source):
    kept = jnp.where(lax.axis_index(axis) == source, value, 0).astype(value.dtype)
    return lax.psum(kept, axis)


def local(latents, policy_out, w_qkv, w_out, qk_gains, mod_table, timestep, owner):
    held = w_qkv.shape[0]
    local_block = owner[0] % held
    root_group = owner[0] // held
    mine_qkv = lax.dynamic_index_in_dim(w_qkv, local_block, 0, keepdims=False)
    mine_out = lax.dynamic_index_in_dim(w_out, local_block, 0, keepdims=False)
    mine_gains = lax.dynamic_index_in_dim(qk_gains, local_block, 0, keepdims=False)
    weights_qkv, weights_out, gains = (
        spread_2(mine_qkv, "own", root_group),
        spread_2(mine_out, "own", root_group),
        spread_2(mine_gains, "own", root_group),
    )
    rows_here = latents.shape[1]
    part_cols = weights_qkv.shape[2]
    heads_here = part_cols // HD
    onehot = (jnp.arange(mod_table.shape[0], dtype=jnp.int32) == timestep[0]).astype(jnp.float32)
    modulation = jnp.tensordot(onehot, mod_table, axes=1, precision=lax.Precision.HIGHEST)
    shift, scale, gate = (modulation[0], modulation[1], modulation[2])
    inputs = latents[0].astype(jnp.float32)
    center = jnp.mean(inputs, axis=-1, keepdims=True)
    spread = jnp.mean((inputs - center) ** 2, axis=-1, keepdims=True)
    normed = (inputs - center) * lax.rsqrt(spread + 1e-06)
    modulated = (normed * (1.0 + scale) + shift).astype(jnp.bfloat16)
    piece = lax.all_gather(weights_qkv, "seq", axis=0, tiled=True)
    qkv = jnp.dot(
        modulated, piece.reshape(piece.shape[0], 3 * part_cols), preferred_element_type=jnp.float32
    )
    qkv = qkv.reshape(rows_here, 3, part_cols)
    query, key, value = (qkv[:, 0], qkv[:, 1], qkv[:, 2])
    query_sq, key_sq = lax.psum(
        (jnp.sum(query * query, axis=-1), jnp.sum(key * key, axis=-1)), "tp"
    )
    gains_f = gains.astype(jnp.float32)
    query = (query * lax.rsqrt(query_sq / HW + 1e-06)[:, None] * gains_f[0]).astype(jnp.bfloat16)
    key = (key * lax.rsqrt(key_sq / HW + 1e-06)[:, None] * gains_f[1]).astype(jnp.bfloat16)
    value = value.astype(jnp.bfloat16)
    query = query.reshape(rows_here, heads_here, HD)
    key = key.reshape(rows_here, heads_here, HD)
    value = value.reshape(rows_here, heads_here, HD)
    run_max = jnp.full((heads_here, rows_here), -1e30, jnp.float32)
    key_piece = lax.all_gather(key, ("own", "seq"), axis=0, tiled=True)
    value_piece = lax.all_gather(value, ("own", "seq"), axis=0, tiled=True)
    scores = jnp.einsum("qhd,khd->hqk", query, key_piece, preferred_element_type=jnp.float32) * (
        1.0 / HD**0.5
    )
    new_max = jnp.maximum(run_max, jnp.max(scores, axis=-1))
    probs = jnp.exp(scores - new_max[:, :, None])
    new_sum = jnp.sum(probs, axis=-1)
    mixed = jnp.einsum(
        "hqk,khd->hqd", probs.astype(jnp.bfloat16), value_piece, preferred_element_type=jnp.float32
    )
    attn = (mixed / new_sum[:, :, None]).astype(jnp.bfloat16)
    attn = attn.transpose(1, 0, 2).reshape(rows_here, part_cols)
    proj = jnp.dot(
        attn,
        lax.all_gather(weights_out, "seq", axis=1, tiled=True),
        preferred_element_type=jnp.float32,
    )
    share = lax.psum_scatter(
        proj.astype(jnp.bfloat16), "tp", scatter_dimension=1, tiled=True
    ).astype(jnp.float32)
    share_cols = share.shape[1]
    offset = lax.axis_index("tp") * share_cols
    inputs_part = lax.dynamic_slice_in_dim(inputs, offset, share_cols, 1)
    gate_part = lax.dynamic_slice_in_dim(gate, offset, share_cols, 0)
    block = (inputs_part + gate_part * share).astype(jnp.bfloat16)
    differ = block.astype(jnp.float32) - policy_out[0].astype(jnp.float32)
    squares = lax.psum(jnp.sum(differ * differ, axis=-1), "tp") / D
    return (block[None], squares[None])


def solution(mesh):
    placed = (
        P(None, ("own", "seq"), None),
        P(None, ("own", "seq"), "tp"),
        P("own", "seq", None, "tp"),
        P("own", "tp", "seq"),
        P("own", None, "tp"),
        P(),
        P(),
        P(),
    )
    return jax.shard_map(
        local,
        mesh=mesh,
        in_specs=placed,
        out_specs=(P(None, ("own", "seq"), "tp"), P(None, ("own", "seq"))),
        check_vma=False,
    )
```

profile of v0, /device:TPU:1, one launch (start us, length us, event | category | flops | bytes accessed | tf_op | source)
XLA Modules:
  0.0 714.8 jit_solution(9187236233076922170)
XLA Ops:
  7.9 3.4 constant_dynamic-slice_fusion
  11.3 3.9 copy.21
  15.2 1.7 select_bitcast_fusion
  16.9 2.3 select_bitcast_fusion.1
  19.2 80.9 %all-reduce.4.cloned.1.call-done = (bf16[640,3,640]{0,2,1:T(8,128)(2,1)}, bf16[640,640]{1,0:T(8,128)(2,1)}) async-done(((bf16[640,3,640]{0,2,1:T(8,128)(2,1)}, bf16[640,640]{1,0:T(8,128)(2,1)}), (bf16[640,3,640]{0,2,1:T(8,128)(2,1)}, bf16[640,640]{1,0:T(8,128)(2,1)})) %all-reduce.4.cloned.1.call-update) | async-done | bytes 3276816 | tf_op jit(solution)/shard_map/psum | solution.py:13
  101.2 0.7 fusion.31
  101.9 6.6 psum.44
  109.0 0.8 fusion.9
  109.9 199.7 %all-gather.5.cloned.1.call-done = bf16[5120,3,640]{0,2,1:T(8,128)(2,1)} async-done(((bf16[640,3,640]{0,2,1:T(8,128)(2,1)}), bf16[5120,3,640]{0,2,1:T(8,128)(2,1)}) %all-gather.5.cloned.1.call-update) | async-done | bytes 19660816 | tf_op jit(solution)/shard_map/all_gather | solution.py:39
  309.6 10.9 %fusion.6 = f32[256,3,640]{2,0,1:T(8,128)S(1)} fusion(bf16[5120,3,640]{0,2,1:T(8,128)(2,1)} %all-gather.5.cloned.1.call-done, bf16[1,256,5120]{2,1,0:T(8,128)(2,1)S(1)} %copy-done.2, f32[5120]{0:T(1024)S(1)} %bitcast.74, f32[5120]{0:T(1024)S(1)} %bitcast.75, f32[256]{0:T(256)S(1)} %add_rsqrt_fusion.2, f32[256]{0:T(256)S(1)} %broadcast_multiply_fusion.1), kind=kOutput, calls=%fused_computation.7 | convolution fusion | flops 5041029120 | bytes 24291328 | tf_op jit(solution)/shard_map/dot_general | solution.py:40
  320.5 1.3 copy-done.3
  321.8 1.2 multiply_reduce_fusion.2
  323.0 6.4 all-reduce
  329.4 2.2 copy.15
  331.5 2.2 copy.16
  333.7 2.0 multiply_convert_fusion
  335.7 1.1 slice.47
  336.9 0.9 copy.18
  337.9 0.5 all-gather.11.cloned.1.call-update
  338.6 2.2 copy.14
  340.8 108.0 %all-gather.7.cloned.1.call-done = bf16[8192,5,128]{2,0,1:T(8,128)(2,1)} async-done(((bf16[256,5,128]{2,0,1:T(8,128)(2,1)}), bf16[8192,5,128]{2,0,1:T(8,128)(2,1)}) %all-gather.7.cloned.1.call-update) | async-done | bytes 10485776 | tf_op jit(solution)/shard_map/all_gather | solution.py:56
  448.8 19.2 %multiply_reduce_fusion = (f32[5,256]{1,0:T(8,128)S(1)}, f32[5,256,8192]{2,1,0:T(8,128)}) fusion(bf16[8192,5,128]{2,0,1:T(8,128)(2,1)} %all-gather.7.cloned.1.call-done, f32[256,5,128]{0,2,1:T(8,128)} %bitcast.67, f32[5,128]{1,0:T(8,128)S(1)} %bitcast.73, f32[256]{0:T(256)S(1)} %add_rsqrt_fusion.1), kind=kOutput, calls=%fused_computation.1 | convolution fusion | flops 2705816320 | bytes 53092864 | tf_op jit(solution)/shard_map/qhd,khd->hqk/dot_general | solution.py:58
  468.0 17.5 %fusion = f32[5,256]{1,0:T(8,128)S(1)} fusion(f32[5,256,8192]{2,1,0:T(8,128)} %get-tuple-element.18, f32[5,256]{1,0:T(8,128)S(1)} %broadcast_maximum_fusion), kind=kLoop, calls=%fused_computation.2 | loop fusion | flops 31456000 | bytes 41953280 | tf_op jit(solution)/shard_map/reduce_sum | solution.py:63
  485.5 82.8 %all-gather.9.cloned.1.call-done = bf16[8192,5,128]{0,2,1:T(8,128)(2,1)} async-done(((bf16[256,5,128]{0,2,1:T(8,128)(2,1)}), bf16[8192,5,128]{0,2,1:T(8,128)(2,1)}) %all-gather.9.cloned.1.call-update) | async-done | bytes 10485776 | tf_op jit(solution)/shard_map/all_gather | solution.py:57
  568.2 20.0 %fusion.25 = bf16[256,5,128]{0,2,1:T(8,128)(2,1)S(1)} fusion(bf16[8192,5,128]{0,2,1:T(8,128)(2,1)} %all-gather.9.cloned.1.call-done, f32[5,256,8192]{2,1,0:T(8,128)} %get-tuple-element.18, f32[5,256]{1,0:T(8,128)S(1)} %broadcast_maximum_fusion, f32[256,5]{0,1:T(8,128)S(1)} %bitcast.71), kind=kOutput, calls=%fused_computation.28 | convolution fusion | flops 2716139520 | bytes 52766720 | tf_op jit(solution)/shard_map/hqk,khd->hqd/dot_general | solution.py:64
  588.2 73.0 %all-gather.11.cloned.1.call-done = bf16[640,5120]{1,0:T(8,128)(2,1)} async-done(((bf16[640,640]{1,0:T(8,128)(2,1)}), bf16[640,5120]{1,0:T(8,128)(2,1)}) %all-gather.11.cloned.1.call-update) | async-done | bytes 6553616 | tf_op jit(solution)/shard_map/all_gather | solution.py:71
  661.3 6.6 convolution_convert_fusion
  667.9 2.9 convert_element_type.61
  670.8 28.4 %reduce-scatter.2.cloned.1.call-done = bf16[256,1280]{1,0:T(8,128)(2,1)} async-done(((bf16[256,5120]{1,0:T(8,128)(2,1)}), bf16[256,1280]{1,0:T(8,128)(2,1)}) %reduce-scatter.2.cloned.1.call-update) | async-done | bytes 655376 | tf_op jit(solution)/shard_map/reduce_scatter | solution.py:74
  699.2 2.9 fusion.17
  702.1 5.3 psum.47
  707.4 0.6 broadcast_multiply_fusion
  (30 shorter events, 1.5 us)
Async XLA Ops:
  7.2 93.7 %copy-start = (f32[8,3,5120]{2,0,1:T(8,128)S(1)}, f32[8,3,5120]{2,0,1:T(8,128)}, u32[]{:S(2)}) copy-start(f32[8,3,5120]{2,0,1:T(8,128)} %param.13) | copy-start | bytes 1474564
  7.2 92.9 %all-reduce.4.cloned.1.call-start = ((), (), s32[]{:S(2)}) async-start(), calls=%async_computation.6 | async-start | bytes 6553600 | tf_op jit(solution)/shard_map/psum | solution.py:13
  16.9 91.7 %copy-start.2 = (bf16[1,256,5120]{2,1,0:T(8,128)(2,1)S(1)}, bf16[1,256,5120]{2,1,0:T(8,128)(2,1)}, u32[]{:S(2)}) copy-start(bf16[1,256,5120]{2,1,0:T(8,128)(2,1)} %param.8) | copy-start | bytes 7864324
  19.1 290.5 %all-gather.5.cloned.1.call-start = ((), (), s32[]{:S(2)}) async-start(), calls=%async_computation.1 | async-start | bytes 22118400 | tf_op jit(solution)/shard_map/all_gather | solution.py:39
  100.1 348.6 %all-gather.7.cloned.1.call-start = ((), (), s32[]{:S(2)}) async-start(), calls=%async_computation.2 | async-start | bytes 10813440 | tf_op jit(solution)/shard_map/all_gather | solution.py:56
  320.5 1.3 copy-start.3
  335.7 232.6 %all-gather.9.cloned.1.call-start = ((), (), s32[]{:S(2)}) async-start(), calls=%async_computation.3 | async-start | bytes 10813440 | tf_op jit(solution)/shard_map/all_gather | solution.py:57
  337.8 323.4 %all-gather.11.cloned.1.call-start = ((), (), s32[]{:S(2)}) async-start(), calls=%async_computation.4 | async-start | bytes 7372800 | tf_op jit(solution)/shard_map/all_gather | solution.py:71
  338.4 360.8 %reduce-scatter.2.cloned.1.call-start = ((), (), s32[]{:S(2)}) async-start(), calls=%async_computation.5 | async-start | bytes 3276800 | tf_op jit(solution)/shard_map/reduce_scatter | solution.py:74
  667.9 40.1 %copy-start.1 = (f32[8,3,5120]{2,0,1:T(8,128)S(1)}, f32[8,3,5120]{2,0,1:T(8,128)}, u32[]{:S(2)}) copy-start(f32[8,3,5120]{2,0,1:T(8,128)} %param.13) | copy-start | bytes 1474564
Sparse Core Ops, SparseCore 0:
  19.3 80.8 all-reduce.3
  102.5 207.0 all-gather.4
  335.8 112.9 all-gather.6
  451.4 116.7 all-gather.8
  570.5 90.6 all-gather.10
  668.0 31.1 reduce-scatter.1
where the time goes:
time: 716 us; the launch traced here: 715 us
  waiting for transfers between devices  573 us (80%)
  matrix products  57 us (8%)
  other arithmetic  33 us (5%)
  blocking collectives  18.3 us (3%)
  local copies, waits for them, and re-layouts  17.1 us (2%)
  between operations  15.6 us (2%)
    all_gather x1, waiting for transfers between devices, local(): piece = lax.all_gather(weights_qkv, 'seq', axis=0, tiled=True)  200 us
    all_gather x1, waiting for transfers between devices, local(): key_piece = lax.all_gather(key, ('own', 'seq'), axis=0, tiled=True)  108 us
    all_gather x1, waiting for transfers between devices, local(): value_piece = lax.all_gather(value, ('own', 'seq'), axis=0, tiled=True)  82.8 us
    psum x1, waiting for transfers between devices, spread_2(): return lax.psum(kept, axis)  80.9 us
    all_gather x1, waiting for transfers between devices, local(): lax.all_gather(weights_out, 'seq', axis=1, tiled=True)  73 us
    reduce_scatter x1, waiting for transfers between devices, local(): lax.psum_scatter(proj.astype(jnp.bfloat16), 'tp', scatter_dimension=1, ti...  28.4 us
    dot_general x1, matrix products, local(): jnp.einsum('hqk,khd->hqd', probs.astype(jnp.bfloat16), value_piece, prefe...  20 us
    dot_general x1, matrix products, local(): jnp.einsum('qhd,khd->hqk', query, key_piece, preferred_element_type=jnp.f...  19.2 us
  transfers between devices with their start and end apart: 6, of which 6 were waited for; matrix products, arithmetic and copies ran while one was open for 9% of the time, Pallas kernels for 0%

commit v1 on v0

v1 whole, which is shorter than its diff:
```python
import jax
import jax.numpy as jnp
from jax import lax
from jax.experimental import pallas as pl
from jax.experimental.pallas import tpu as pltpu
from jax.sharding import PartitionSpec as P

D = 5120
HD = 128
HW = 2560
ROWS = 256
COLS = 640
HEADS_HERE = 5
QUARTER = 160
EPS = 1e-06
MESH = pl.DeviceIdType.MESH
ANY = pl.BlockSpec(memory_space=pl.ANY)
VMEM = pl.BlockSpec(memory_space=pltpu.VMEM)
LIMIT = 62 * 1024 * 1024


def remote(src, dst, send, recv, device):
    return pltpu.make_async_remote_copy(
        src_ref=src, dst_ref=dst, send_sem=send, recv_sem=recv, device_id=device, device_id_type=MESH
    )


def place():
    x, s, tp = lax.axis_index("own"), lax.axis_index("seq"), lax.axis_index("tp")
    return x, s, tp


def spread_kernel(root, w_ref, wo_ref, gain_ref, w_out, wo_out, gain_out, w_mid, wo_mid, gain_mid,
                  send_sem, recv_sem, mid_sem, pass_sem, local_sem):
    x, s, tp = place()
    z, yh = s // 2, s % 2
    far = (root + 2) % 4
    mid = (root + 3) % 4 if ((far ^ 1) - root) % 4 == 1 else (root + 1) % 4

    @pl.when(x == root)
    def _():
        for group in range(4):
            plane = mid if group == far else group
            land = (w_mid, wo_mid, gain_mid) if group == far else (w_out, wo_out, gain_out)
            sems = mid_sem if group == far else recv_sem

            @pl.when(tp == group)
            def _(group=group, plane=plane, land=land, sems=sems):
                for phase in ("start", "wait"):
                    for quarter in range(4):
                        piece = w_ref.at[:, pl.ds(quarter * QUARTER, QUARTER), :]
                        wo_piece = wo_ref.at[pl.ds(quarter * QUARTER, QUARTER), :]
                        near = (plane, s, quarter)
                        wo_dest = (plane, quarter * 2 + yh, z)
                        if plane == root and quarter == group:
                            copies = [
                                pltpu.make_async_copy(piece, land[0], local_sem.at[0]),
                                pltpu.make_async_copy(gain_ref, land[2], local_sem.at[2]),
                            ]
                        else:
                            copies = [
                                remote(piece, land[0], send_sem.at[quarter], sems.at[0], near),
                                remote(gain_ref, land[2], send_sem.at[8 + quarter], sems.at[2], near),
                            ]
                        for copy in copies:
                            if phase == "start":
                                copy.start()
                            elif plane == root and quarter == group:
                                copy.wait()
                            else:
                                copy.wait_send()
                        far_wo = remote(wo_piece, land[1], send_sem.at[4 + quarter], sems.at[1], wo_dest)
                        if plane == root:
                            here = (z == group) & (z == quarter)

                            @pl.when(here)
                            def _(wo_piece=wo_piece, land=land, phase=phase):
                                copy = pltpu.make_async_copy(wo_piece, land[1], local_sem.at[1])
                                copy.start() if phase == "start" else copy.wait()

                            @pl.when(jnp.logical_not(here))
                            def _(far_wo=far_wo, phase=phase):
                                far_wo.start() if phase == "start" else far_wo.wait_send()
                        else:
                            far_wo.start() if phase == "start" else far_wo.wait_send()

    @pl.when(x == mid)
    def _():
        target = (far, s, tp)
        hops = []
        for i, (held, land) in enumerate(((w_mid, w_out), (wo_mid, wo_out), (gain_mid, gain_out))):
            remote(held, held, pass_sem.at[i], mid_sem.at[i], target).wait_recv()
            hop = remote(held, land, pass_sem.at[i], recv_sem.at[i], target)
            hop.start()
            hops.append(hop)
        for hop in hops:
            hop.wait_send()

    def arrive(i, ref):
        remote(ref, ref, send_sem.at[0], recv_sem.at[i], (x, s, tp)).wait_recv()

    at_root = x == root

    @pl.when(jnp.logical_not(at_root & (tp == root)))
    def _():
        arrive(0, w_out)
        arrive(2, gain_out)

    @pl.when(jnp.logical_not(at_root & (tp == root) & (z == root)))
    def _():
        arrive(1, wo_out)


def spread(root, w, wo, gain):
    shapes = [(3, QUARTER, COLS), (QUARTER, COLS), (16, COLS)]
    return pl.pallas_call(
        lambda *refs: spread_kernel(root, *refs),
        out_shape=[jax.ShapeDtypeStruct(shape, jnp.bfloat16) for shape in shapes],
        in_specs=[ANY] * 3,
        out_specs=[ANY] * 3,
        scratch_shapes=[pltpu.VMEM(shape, jnp.bfloat16) for shape in shapes]
        + [
            pltpu.SemaphoreType.DMA((12,)),
            pltpu.SemaphoreType.DMA((3,)),
            pltpu.SemaphoreType.DMA((3,)),
            pltpu.SemaphoreType.DMA((3,)),
            pltpu.SemaphoreType.DMA((3,)),
        ],
        compiler_params=pltpu.CompilerParams(has_side_effects=True, vmem_limit_bytes=16 * 1024 * 1024),
        name=f"spread_{root}",
    )(w, wo, gain)


class Gather:
    def __init__(self, own, slot, dest, half, send_sem, recv_sem, pair_sem):
        self.x, s, tp = place()
        core, yl = tp % 2, tp // 2
        z, y = s // 2, (s % 2) * 2 + yl
        self.core, self.z, self.y = core, z, y
        self.own, self.slot, self.dest, self.half = own, slot, dest, half
        self.send_sem, self.recv_sem, self.pair_sem = send_sem, recv_sem, pair_sem
        self.sent = []

        def device(dz, dy):
            z2, y2 = (z + dz) % 4, (y + dy) % 4
            return (self.x, z2 * 2 + y2 // 2, (y2 % 2) * 2 + core)

        self.first = {d: device((1 - core) * d, core * d) for d in (1, 3)}
        self.second = {d: device(core * d, (1 - core) * d) for d in (1, 3)}
        self.sibling = (self.x, s, tp + 1 - 2 * core)
        self.recv_index = {(1, 0): 0, (3, 0): 1, (2, 0): 2}
        for k in range(4):
            self.recv_index[(k, 1)] = 4 + 4 * k
            self.recv_index[(k, 3)] = 5 + 4 * k
            self.recv_index[(k, 2)] = 6 + 4 * k

    def push(self, src, dst, recv, device):
        copy = remote(src, dst, self.send_sem.at[len(self.sent)], recv, device)
        copy.start()
        self.sent.append(copy)

    def to_sibling(self, k, j, src=None):
        src = self.slot(0, k, j) if src is None else src
        self.push(src, self.dest(1, k, j, k, j), self.pair_sem.at[4 * k + j], self.sibling)

    def along_second(self, k, src=None):
        src = self.slot(0, k, 0) if src is None else src
        for d in (1, 3):
            j = (0 - d) % 4
            self.push(src, self.dest(0, k, 0, k, j), self.recv_sem.at[self.recv_index[(k, j)]], self.second[d])

    def begin(self):
        for d in (1, 3):
            k = (0 - d) % 4
            self.push(self.own, self.dest(0, 0, 0, k, 0), self.recv_sem.at[self.recv_index[(k, 0)]], self.first[d])
        self.along_second(0, self.own)
        self.to_sibling(0, 0, self.own)

    def take(self, ref, sem):
        remote(ref, ref, self.send_sem.at[0], sem, self.sibling).wait_recv()

    def first_near(self, k):
        self.take(self.slot(0, k, 0), self.recv_sem.at[self.recv_index[(k, 0)]])
        h, d = (0, 1) if k == 3 else (1, 3)
        self.push(
            self.half(self.slot(0, k, 0), h), self.half(self.dest(0, k, 0, 2, 0), h),
            self.recv_sem.at[self.recv_index[(2, 0)] + h], self.first[d],
        )
        self.along_second(k)
        self.to_sibling(k, 0)

    def first_far(self):
        for h in range(2):
            self.take(self.half(self.slot(0, 2, 0), h), self.recv_sem.at[self.recv_index[(2, 0)] + h])
        self.along_second(2)
        self.to_sibling(2, 0)

    def second_near(self, k):
        for j in (3, 1):
            self.take(self.slot(0, k, j), self.recv_sem.at[self.recv_index[(k, j)]])
            h, d = (0, 1) if j == 3 else (1, 3)
            self.push(
                self.half(self.slot(0, k, j), h), self.half(self.dest(0, k, j, k, 2), h),
                self.recv_sem.at[self.recv_index[(k, 2)] + h], self.second[d],
            )
            self.to_sibling(k, j)

    def second_far(self, k):
        for h in range(2):
            self.take(self.half(self.slot(0, k, 2), h), self.recv_sem.at[self.recv_index[(k, 2)] + h])
        self.to_sibling(k, 2)

    def from_sibling(self, k, j):
        self.take(self.slot(1, k, j), self.pair_sem.at[4 * k + j])

    def finish(self):
        for copy in self.sent:
            copy.wait_send()


GATHER_SEMS = [
    pltpu.SemaphoreType.DMA((36,)),
    pltpu.SemaphoreType.DMA((20,)),
    pltpu.SemaphoreType.DMA((16,)),
]


def qkv_kernel(xm_ref, w_ref, wo_ref, gain_ref, q_out, kv_out, wo_out,
               wbuf, xbuf, acc, sums, send_sem, recv_sem, pair_sem, x_send, x_recv, x_local,
               wo_send, wo_recv, wo_local, sum_send, sum_recv):
    x, s, tp = place()
    core = tp % 2
    z, yh = s // 2, s % 2
    a0 = z * (1 - core) + ((s % 2) * 2 + tp // 2) * core
    b0 = z * core + ((s % 2) * 2 + tp // 2) * (1 - core)

    def slot(pair, k, j):
        if pair:
            a, b, kind = (b0 + k) % 4, (a0 + j) % 4, 1 - core
        else:
            a, b, kind = (a0 + k) % 4, (b0 + j) % 4, core
        z2 = a * (1 - kind) + b * kind
        y2 = a * kind + b * (1 - kind)
        offset = pl.multiple_of(((y2 % 2) * 2 + kind) * QUARTER, 32)
        return wbuf.at[:, z2 * 2 + y2 // 2, pl.ds(offset, QUARTER), :]

    def dest(pair, k, j, k2, j2):
        return slot(0, k, j)

    def half(ref, h):
        return ref.at[:, pl.ds(h * (QUARTER // 2), QUARTER // 2), :]

    gather = Gather(w_ref, slot, dest, half, send_sem, recv_sem, pair_sem)
    gather.begin()
    own_w = pltpu.make_async_copy(w_ref, slot(0, 0, 0), x_local.at[4])
    own_w.start()

    turn = (x - tp) % 4
    chunk = ROWS // 4
    part = [pl.ds(i * chunk, chunk) for i in range(4)]
    up, down = ((x + 1) % 4, s, tp), ((x + 3) % 4, s, tp)

    def x_send_copy(i, n, device, src):
        return remote(src.at[part[i]], xbuf.at[part[i]], x_send.at[4 * n + i], x_recv.at[i], device)

    @pl.when(turn == 0)
    def _():
        for i in range(4):
            x_send_copy(i, 0, up, xm_ref).start()
            x_send_copy(i, 1, down, xm_ref).start()
            pltpu.make_async_copy(xm_ref.at[part[i]], xbuf.at[part[i]], x_local.at[i]).start()

    relay = turn == 3 - 2 * core
    onward = ((x + 3 + 2 * core) % 4, s, tp)

    def pass_tokens():
        @pl.when(relay)
        def _():
            for i in range(4):
                x_send_copy(i, 0, onward, xbuf).wait_recv()
                x_send_copy(i, 0, onward, xbuf).start()

    def need_tokens():
        @pl.when(turn == 0)
        def _():
            for i in range(4):
                pltpu.make_async_copy(xm_ref.at[part[i]], xbuf.at[part[i]], x_local.at[i]).wait()

        @pl.when((turn != 0) & jnp.logical_not(relay))
        def _():
            for i in range(4):
                x_send_copy(i, 0, up, xbuf).wait_recv()

    acc[...] = jnp.zeros_like(acc)
    gather.first_near(3)
    gather.first_near(1)
    gather.second_near(0)
    gather.first_far()
    gather.second_near(3)
    pass_tokens()
    gather.second_far(0)

    def wo_place(z2, yh2):
        return wo_out.at[pl.ds(pl.multiple_of(z2 * QUARTER, 32), QUARTER), pl.ds(pl.multiple_of(yh2 * COLS, 128), COLS)]

    def wo_copy(i, dz, dy):
        device = (x, ((z + dz) % 4) * 2 + (yh + dy) % 2, tp)
        return remote(wo_ref, wo_place(z, yh), wo_send.at[i], wo_recv.at[i], device)

    offsets = [(1, 0), (3, 0), (0, 1), (1, 1), (3, 1), (2, 0), (2, 1)]

    def dots(first, count):
        def body(i, carry):
            z2 = (z + first + 2 * (i // 2)) % 4
            row = z2 * 2 + i % 2
            tokens = xbuf[:, pl.ds(pl.multiple_of(row * COLS, 128), COLS)]
            for j in range(3):
                acc[j] += jnp.dot(tokens, wbuf[j, row], preferred_element_type=jnp.float32)
            return carry

        lax.fori_loop(0, count, body, 0)

    own_w.wait()
    seen = set()

    def siblings(limit):
        for k in range(4):
            for j in range(4):
                if (k in limit or j in limit) and (k, j) not in seen:
                    seen.add((k, j))
                    gather.from_sibling(k, j)

    gather.second_near(1)
    gather.second_far(3)
    gather.second_near(2)
    siblings((0,))
    need_tokens()
    dots(0, 2)
    gather.second_far(1)
    for i, (dz, dy) in enumerate(offsets):
        wo_copy(i, dz, dy).start()
    own_wo = pltpu.make_async_copy(wo_ref, wo_place(z, yh), wo_local)
    own_wo.start()
    siblings((1, 3))
    dots(1, 4)
    gather.second_far(2)
    siblings((2,))
    dots(2, 2)

    query, key = acc[0], acc[1]
    lane = lax.broadcasted_iota(jnp.int32, (ROWS, 128), 1)
    sums[0] = jnp.where(
        lane == 0, jnp.sum(query * query, axis=1, keepdims=True), jnp.sum(key * key, axis=1, keepdims=True)
    )
    kv_out[:, COLS:] = acc[2].astype(jnp.bfloat16)
    shares = [remote(sums.at[0], sums.at[d], sum_send.at[d], sum_recv.at[d], ((x + d) % 4, s, tp)) for d in (1, 2, 3)]
    for share in shares:
        share.start()
    gains = gain_ref[...].astype(jnp.float32)
    for share in shares:
        share.wait()
    total = (sums[0] + sums[1]) + (sums[2] + sums[3])
    scale = lax.rsqrt(total / HW + EPS)
    q_out[...] = (acc[0] * scale[:, 0:1] * gains[0:1]).astype(jnp.bfloat16)
    kv_out[:, :COLS] = (acc[1] * scale[:, 1:2] * gains[1:2]).astype(jnp.bfloat16)

    @pl.when(turn == 0)
    def _():
        for i in range(4):
            x_send_copy(i, 0, up, xm_ref).wait_send()
            x_send_copy(i, 1, down, xm_ref).wait_send()

    @pl.when(relay)
    def _():
        for i in range(4):
            x_send_copy(i, 0, onward, xbuf).wait_send()

    for i, (dz, dy) in enumerate(offsets):
        copy = wo_copy(i, dz, dy)
        copy.wait_send()
        z2, yh2 = (z + 4 - dz) % 4, (yh + dy) % 2
        remote(wo_ref, wo_place(z2, yh2), wo_send.at[i], wo_recv.at[i], (x, s, tp)).wait_recv()
    own_wo.wait()
    gather.finish()


def qkv_call(xm, w, wo, gain):
    return pl.pallas_call(
        qkv_kernel,
        out_shape=[
            jax.ShapeDtypeStruct((ROWS, COLS), jnp.bfloat16),
            jax.ShapeDtypeStruct((ROWS, 2 * COLS), jnp.bfloat16),
            jax.ShapeDtypeStruct((COLS, 2 * COLS), jnp.bfloat16),
        ],
        in_specs=[ANY, ANY, ANY, VMEM],
        out_specs=[VMEM, VMEM, ANY],
        scratch_shapes=[
            pltpu.VMEM((3, 8, COLS, COLS), jnp.bfloat16),
            pltpu.VMEM((ROWS, D), jnp.bfloat16),
            pltpu.VMEM((3, ROWS, COLS), jnp.float32),
            pltpu.VMEM((4, ROWS, 128), jnp.float32),
            *GATHER_SEMS,
            pltpu.SemaphoreType.DMA((8,)),
            pltpu.SemaphoreType.DMA((4,)),
            pltpu.SemaphoreType.DMA((5,)),
            pltpu.SemaphoreType.DMA((7,)),
            pltpu.SemaphoreType.DMA((7,)),
            pltpu.SemaphoreType.DMA,
            pltpu.SemaphoreType.DMA((4,)),
            pltpu.SemaphoreType.DMA((4,)),
        ],
        compiler_params=pltpu.CompilerParams(has_side_effects=True, vmem_limit_bytes=LIMIT),
        name="qkv",
    )(xm, w, wo, gain)


def attend_kernel(q_ref, kv_ref, wo_ref, inputs_ref, policy_ref, gate_ref, block_out, err_out,
                  kvbuf, wofull, acc, top, low, attn, pair_attn, afull, errs,
                  send_sem, recv_sem, pair_sem, wo_send, wo_recv, local_sem,
                  a_send, a_recv, a_pair_send, a_pair_recv, y_send, y_recv, e_send, e_recv):
    x, s, tp = place()
    core = tp % 2

    def slot(pair, k, j):
        return kvbuf.at[pair, 4 * k + j]

    def dest(pair, k, j, k2, j2):
        return kvbuf.at[pair, 4 * k2 + j2]

    def half(ref, h):
        return ref.at[pl.ds(h * (ROWS // 2), ROWS // 2), :]

    gather = Gather(kv_ref, slot, dest, half, send_sem, recv_sem, pair_sem)
    gather.begin()
    own_kv = pltpu.make_async_copy(kv_ref, slot(0, 0, 0), local_sem.at[0])
    own_kv.start()

    up, down = ((x + 1) % 4, s, tp), ((x + 3) % 4, s, tp)
    rows = [pl.ds(0, COLS // 2), pl.ds(COLS // 2, COLS // 2)]

    def wo_copy(i, src, plane, h, device, n):
        return remote(src, wofull.at[plane, rows[h]], wo_send.at[i], wo_recv.at[n], device)

    own_sends = [
        wo_copy(0, wo_ref.at[rows[0]], x, 0, up, 0),
        wo_copy(1, wo_ref.at[rows[1]], x, 1, down, 1),
        wo_copy(2, wo_ref.at[rows[1]], x, 1, up, 2),
        wo_copy(3, wo_ref.at[rows[0]], x, 0, down, 3),
    ]
    for copy in own_sends:
        copy.start()
    own_wo = pltpu.make_async_copy(wo_ref, wofull.at[x], local_sem.at[1])
    own_wo.start()
    below, above, across = (x + 3) % 4, (x + 1) % 4, (x + 2) % 4
    onward = [
        wo_copy(4, wofull.at[below, rows[0]], below, 0, up, 4),
        wo_copy(5, wofull.at[above, rows[1]], above, 1, down, 5),
    ]

    def pass_wo():
        wo_copy(4, wofull.at[below, rows[0]], below, 0, up, 0).wait_recv()
        onward[0].start()
        wo_copy(5, wofull.at[above, rows[1]], above, 1, down, 1).wait_recv()
        onward[1].start()

    def need_wo():
        own_wo.wait()
        wo_copy(2, wo_ref.at[rows[1]], below, 1, up, 2).wait_recv()
        wo_copy(3, wo_ref.at[rows[0]], above, 0, up, 3).wait_recv()
        wo_copy(4, wo_ref.at[rows[0]], across, 0, up, 4).wait_recv()
        wo_copy(5, wo_ref.at[rows[1]], across, 1, up, 5).wait_recv()

    acc[...] = jnp.zeros_like(acc)
    low[...] = jnp.zeros_like(low)
    top[...] = jnp.full_like(top, -1e30)
    factor = float(HD) ** -0.5 * 1.4426950408889634

    def flash(pair, k):
        def body(h, carry):
            cols = pl.ds(pl.multiple_of(h * HD, HD), HD)
            vcols = pl.ds(pl.multiple_of(COLS + h * HD, HD), HD)
            keys = kvbuf[pair, pl.ds(4 * k, 4), :, cols].reshape(4 * ROWS, HD)
            values = kvbuf[pair, pl.ds(4 * k, 4), :, vcols].reshape(4 * ROWS, HD)
            scores = lax.dot_general(
                q_ref[:, cols], keys, (((1,), (1,)), ((), ())), preferred_element_type=jnp.float32
            )
            old = top[h]
            new = jnp.maximum(old, jnp.max(scores, axis=1, keepdims=True))
            top[h] = new
            decay = jnp.exp2((old - new) * factor)
            probs = jnp.exp2((scores - new[:, 0:1]) * factor)
            part = probs[:, 0:128]
            for i in range(1, 4 * ROWS // 128):
                part = part + probs[:, i * 128 : (i + 1) * 128]
            low[h] = low[h] * decay + part
            acc[h] = acc[h] * decay + jnp.dot(
                probs.astype(jnp.bfloat16), values, preferred_element_type=jnp.float32
            )
            return carry

        lax.fori_loop(0, HEADS_HERE, body, 0)

    def siblings(k):
        for j in range(4):
            gather.from_sibling(k, j)

    gather.first_near(3)
    gather.first_near(1)
    gather.second_near(0)
    gather.first_far()
    gather.second_near(3)
    pass_wo()
    own_kv.wait()
    gather.second_far(0)
    flash(0, 0)
    gather.second_near(1)
    gather.second_far(3)
    siblings(0)
    flash(1, 0)
    flash(0, 3)
    gather.second_near(2)
    gather.second_far(1)
    siblings(3)
    flash(1, 3)
    flash(0, 1)
    gather.second_far(2)
    siblings(1)
    flash(1, 1)
    siblings(2)
    flash(0, 2)
    flash(1, 2)

    for h in range(HEADS_HERE):
        total = jnp.sum(low[h], axis=1, keepdims=True)
        attn[:, h * HD : (h + 1) * HD] = (acc[h] / total).astype(jnp.bfloat16)
    need_wo()

    partner = (tp + 2) % 4
    swap = remote(attn, pair_attn, y_send, y_recv, (x, s, partner))
    swap.start()

    def deliver(i, block, held, phase):
        near = pltpu.make_async_copy(held, afull.at[x], local_sem.at[2 + i])
        away = remote(held, afull.at[x], a_send.at[i], a_recv.at[x], (block, s, tp))

        @pl.when(x == block)
        def _():
            near.start() if phase == 0 else None

        @pl.when(x != block)
        def _():
            away.start() if phase == 0 else away.wait_send()

    deliver(0, tp, attn, 0)
    swap.wait_recv()
    deliver(1, partner, pair_attn, 0)

    mine = x % 2 == core
    sibling = (x, s, tp + 1 - 2 * core)
    proj = None
    for d in (0, 1, 3, 2):
        plane = (x + d) % 4
        pair_copy = remote(afull.at[plane], afull.at[plane], a_pair_send.at[d], a_pair_recv.at[d], sibling)

        @pl.when(mine)
        def _(d=d, plane=plane, pair_copy=pair_copy):
            if d == 0:
                @pl.when(x == tp)
                def _():
                    pltpu.make_async_copy(attn, afull.at[x], local_sem.at[2]).wait()

                @pl.when(x != tp)
                def _():
                    pltpu.make_async_copy(pair_attn, afull.at[x], local_sem.at[3]).wait()
            else:
                remote(attn, afull.at[plane], a_send.at[0], a_recv.at[plane], sibling).wait_recv()
            pair_copy.start()

        @pl.when(jnp.logical_not(mine))
        def _(pair_copy=pair_copy):
            pair_copy.wait_recv()

        term = jnp.dot(afull[plane], wofull[plane], preferred_element_type=jnp.float32)
        proj = term if proj is None else proj + term

    block = (inputs_ref[...].astype(jnp.float32) + gate_ref[0:1] * proj).astype(jnp.bfloat16)
    block_out[...] = block
    differ = block.astype(jnp.float32) - policy_ref[...].astype(jnp.float32)
    errs[0] = jnp.broadcast_to(jnp.sum(differ * differ, axis=1, keepdims=True), (ROWS, 128))
    for i in range(2):
        deliver(i, (tp, partner)[i], (attn, pair_attn)[i], 1)
    swap.wait_send()

    @pl.when(mine)
    def _():
        for d in range(4):
            plane = (x + d) % 4
            remote(afull.at[plane], afull.at[plane], a_pair_send.at[d], a_pair_recv.at[d], sibling).wait_send()

    shares = [remote(errs.at[0], errs.at[d], e_send.at[d], e_recv.at[d], (x, s, (tp + d) % 4)) for d in (1, 2, 3)]
    for share in shares:
        share.start()
    for copy in own_sends + onward:
        copy.wait_send()
    gather.finish()
    for share in shares:
        share.wait()
    err_out[...] = ((errs[0] + errs[1]) + (errs[2] + errs[3])) / D


def attend_call(q, kv, wo, inputs, policy, gate):
    return pl.pallas_call(
        attend_kernel,
        out_shape=[
            jax.ShapeDtypeStruct((ROWS, D // 4), jnp.bfloat16),
            jax.ShapeDtypeStruct((ROWS, 128), jnp.float32),
        ],
        in_specs=[VMEM, ANY, ANY, VMEM, VMEM, VMEM],
        out_specs=[VMEM, VMEM],
        scratch_shapes=[
            pltpu.VMEM((2, 16, ROWS, 2 * COLS), jnp.bfloat16),
            pltpu.VMEM((4, COLS, 2 * COLS), jnp.bfloat16),
            pltpu.VMEM((HEADS_HERE, ROWS, HD), jnp.float32),
            pltpu.VMEM((HEADS_HERE, ROWS, HD), jnp.float32),
            pltpu.VMEM((HEADS_HERE, ROWS, HD), jnp.float32),
            pltpu.VMEM((ROWS, COLS), jnp.bfloat16),
            pltpu.VMEM((ROWS, COLS), jnp.bfloat16),
            pltpu.VMEM((4, ROWS, COLS), jnp.bfloat16),
            pltpu.VMEM((4, ROWS, 128), jnp.float32),
            *GATHER_SEMS,
            pltpu.SemaphoreType.DMA((6,)),
            pltpu.SemaphoreType.DMA((6,)),
            pltpu.SemaphoreType.DMA((4,)),
            pltpu.SemaphoreType.DMA((2,)),
            pltpu.SemaphoreType.DMA((4,)),
            pltpu.SemaphoreType.DMA((4,)),
            pltpu.SemaphoreType.DMA((4,)),
            pltpu.SemaphoreType.DMA,
            pltpu.SemaphoreType.DMA,
            pltpu.SemaphoreType.DMA((4,)),
            pltpu.SemaphoreType.DMA((4,)),
        ],
        compiler_params=pltpu.CompilerParams(has_side_effects=True, vmem_limit_bytes=LIMIT),
        name="attend",
    )(q, kv, wo, inputs, policy, gate)


def local(latents, policy_out, w_qkv, w_out, qk_gains, mod_table, timestep, owner):
    held = w_qkv.shape[0]
    local_block = owner[0] % held
    root_group = owner[0] // held
    mine_qkv = lax.dynamic_index_in_dim(w_qkv.transpose(0, 2, 1, 3), local_block, 0, keepdims=False)
    mine_out = lax.dynamic_index_in_dim(w_out, local_block, 0, keepdims=False)
    mine_gains = lax.dynamic_index_in_dim(qk_gains, local_block, 0, keepdims=False)
    mine_gains = jnp.pad(mine_gains, ((0, 14), (0, 0)))
    w, wo, gain = lax.switch(
        root_group,
        [lambda a, b, c, root=root: tuple(spread(root, a, b, c)) for root in range(4)],
        mine_qkv, mine_out, mine_gains,
    )
    onehot = (jnp.arange(mod_table.shape[0], dtype=jnp.int32) == timestep[0]).astype(jnp.float32)
    modulation = jnp.tensordot(onehot, mod_table, axes=1, precision=lax.Precision.HIGHEST)
    shift, scale, gate = (modulation[0], modulation[1], modulation[2])
    inputs = latents[0].astype(jnp.float32)
    center = jnp.mean(inputs, axis=-1, keepdims=True)
    spread_sq = jnp.mean((inputs - center) ** 2, axis=-1, keepdims=True)
    normed = (inputs - center) * lax.rsqrt(spread_sq + EPS)
    modulated = (normed * (1.0 + scale) + shift).astype(jnp.bfloat16)
    q, kv, wo_rows = qkv_call(modulated, w, wo, gain)
    offset = lax.axis_index("tp") * (D // 4)
    inputs_part = lax.dynamic_slice_in_dim(latents[0], offset, D // 4, 1)
    gate_part = jnp.broadcast_to(lax.dynamic_slice_in_dim(gate, offset, D // 4, 0)[None], (8, D // 4))
    block, squares = attend_call(q, kv, wo_rows, inputs_part, policy_out[0], gate_part)
    return (block[None], squares[:, 0][None])


def solution(mesh):
    placed = (
        P(None, ("own", "seq"), None),
        P(None, ("own", "seq"), "tp"),
        P("own", "seq", None, "tp"),
        P("own", "tp", "seq"),
        P("own", None, "tp"),
        P(),
        P(),
        P(),
    )
    return jax.shard_map(
        local,
        mesh=mesh,
        in_specs=placed,
        out_specs=(P(None, ("own", "seq"), "tp"), P(None, ("own", "seq"))),
        check_vma=False,
    )
```

time: 716 us -> 289 us (0.40)
  waiting for transfers between devices: 573 us -> 0 us
  Pallas kernels: 0 us -> 269 us
  matrix products: 57 us -> 0.34 us
  other arithmetic: 33 us -> 5.86 us
  blocking collectives: 18.3 us -> 0 us
  between operations: 15.6 us -> 2.28 us
    all_gather x4 -> x0, waiting for transfers between devices: 464 us -> none  [the longest x1 200 us: local(): piece = lax.all_gather(weights_qkv, 'seq', axis=0, tiled=True)]
    pallas_call x0 -> x3, Pallas kernels: none -> 269 us  [the longest x1 120 us: attend_call(): pl.pallas_call(attend_kernel, out_shape=[jax.ShapeDtypeStruct((ROWS, D //...]
    psum x1 -> x0, waiting for transfers between devices: 80.9 us -> none  [spread_2(): return lax.psum(kept, axis)]
    dot_general x4 -> x0, matrix products: 56.6 us -> none  [the longest x1 20 us: local(): jnp.einsum('hqk,khd->hqd', probs.astype(jnp.bfloat16), value_piece, prefe...]
    reduce_scatter x1 -> x0, waiting for transfers between devices: 28.4 us -> none  [local(): lax.psum_scatter(proj.astype(jnp.bfloat16), 'tp', scatter_dimension=1, ti...]
    reduce_sum x4 -> x1, other arithmetic: 22.4 us -> 0.83 us  [local(): spread_sq = jnp.mean((inputs - center) ** 2, axis=-1, keepdims=True)]
    psum x3 -> x0, blocking collectives: 18.3 us -> none  [the longest x1 6.58 us: spread_2(): return lax.psum(kept, axis)]
  transfers between devices with their start and end apart: 6 -> 0, of which waited for: 6 -> 0; matrix products, arithmetic and copies ran while one was open for 9% -> 0% of each run, Pallas kernels for 0% -> 0%
where the time goes in v1:
time: 289 us
  Pallas kernels  269 us (93%)
  local copies, waits for them, and re-layouts  10.9 us (4%)
  other arithmetic  5.86 us (2%)
    pallas_call x1, Pallas kernels, attend_call(): pl.pallas_call(attend_kernel, out_shape=[jax.ShapeDtypeStruct((ROWS, D //...  120 us
    pallas_call x1, Pallas kernels, qkv_call(): pl.pallas_call(qkv_kernel, out_shape=[jax.ShapeDtypeStruct((ROWS, COLS),...  119 us
    pallas_call x1, Pallas kernels, spread(): pl.pallas_call(lambda *refs: spread_kernel(root, *refs), out_shape=[jax.S...  30.8 us

profile of v1, /device:TPU:1, one launch (start us, length us, event | category | flops | bytes accessed | tf_op | source)
XLA Modules:
  0.0 288.5 jit_solution(1325920861601430580)
XLA Ops:
  0.6 0.0 copy-start
  1.4 1.9 dynamic-slice_bitcast_fusion
  3.3 2.1 dynamic-slice_bitcast_fusion.1
  5.4 0.7 dynamic-slice_bitcast_fusion.3
  6.1 30.8 %conditional.1 = ((bf16[3,160,640]{2,1,0:T(8,128)(2,1)}, bf16[160,640]{1,0:T(8,128)(2,1)S(1)}, bf16[16,640]{1,0:T(8,128)(2,1)S(1)})) conditional(s32[]{:T(128)} %clamp.3, (bf16[3,640,640]{2,1,0:T(8,128)(2,1)S(1)}, bf16[640,640]{1,0:T(8,128)(2,1)}, bf16[16,640]{1,0:T(8,128)(2,1)S(1)}) %tuple.20, ...), branch_computations={%region_2.3_spmd, %region_3.4_spmd, %region_4.5_spmd, %region_5.6_... | conditional | bytes 8 | solution.py:656
  6.1 30.8 %spread_3.1 = (bf16[3,160,640]{2,1,0:T(8,128)(2,1)}, bf16[160,640]{1,0:T(8,128)(2,1)S(1)}, bf16[16,640]{1,0:T(8,128)(2,1)S(1)}) custom-call(bf16[3,640,640]{2,1,0:T(8,128)(2,1)S(1)} %get-tuple-element.33.refs_0_, bf16[640,640]{1,0:T(8,128)(2,1)} %get-tuple-element.34.refs_1_, bf16[16,640]{1,0:T(8,128)(2,1)S(1)} %get-tuple-element.35.refs_2_), custom_call_target="tpu_custom_call" | custom-call | tf_op jit(solution)/shard_map/cond/branch_3_fun/spread_3/pallas_call | solution.py:116
  37.0 0.0 copy-start.1
  37.8 0.0 copy-done
  37.8 0.3 fusion.7
  38.2 2.2 convert_reduce_fusion
  40.4 0.0 copy-done.1
  40.4 0.8 fusion.3
  41.2 2.8 fusion.6.xm_ref
  44.0 118.7 %qkv.1 = (bf16[256,640]{1,0:T(8,128)(2,1)}, bf16[256,1280]{1,0:T(8,128)(2,1)}, bf16[640,1280]{1,0:T(8,128)(2,1)}) custom-call(bf16[256,5120]{1,0:T(8,128)(2,1)} %fusion.6.xm_ref, bf16[3,160,640]{2,1,0:T(8,128)(2,1)} %get-tuple-element.46.w_ref, bf16[160,640]{1,0:T(8,128)(2,1)S(1)} %get-tuple-element.47.wo_ref, bf16[16,640]{1,0:T(8,128)(2,1)S(1)} %get-tuple-element.48.gain_ref), custom_call_target="tpu_custom_call" | custom-call | tf_op jit(solution)/shard_map/qkv/pallas_call | solution.py:388
  162.7 0.6 broadcast_in_dim.7.gate_ref
  163.4 2.0 dynamic-slice_bitcast_fusion.2.inputs_ref
  165.3 119.7 %attend.1 = (bf16[256,1280]{1,0:T(8,128)(2,1)}, f32[256,128]{1,0:T(8,128)}) custom-call(bf16[256,640]{1,0:T(8,128)(2,1)} %get-tuple-element.49.q_ref, bf16[256,1280]{1,0:T(8,128)(2,1)} %get-tuple-element.50.kv_ref, bf16[640,1280]{1,0:T(8,128)(2,1)} %get-tuple-element.51.wo_ref, bf16[256,1280]{1,0:T(8,128)(2,1)} %dynamic-slice_bitcast_fusion.2.inputs_ref, ...), custom_call_target="tpu_custom_call" | custom-call | tf_op jit(solution)/shard_map/attend/pallas_call | solution.py:612
  285.0 1.6 slice_reduce_fusion
  286.6 2.0 copy.28
  (6 shorter events, 0.1 us)
Async XLA Ops:
  0.6 37.1 %copy-start = (f32[8,3,5120]{2,0,1:T(8,128)S(1)}, f32[8,3,5120]{2,0,1:T(8,128)}, u32[]{:S(2)}) copy-start(f32[8,3,5120]{2,0,1:T(8,128)} %param.17) | copy-start | bytes 1474564
  37.0 3.4 %copy-start.1 = (bf16[1,256,5120]{2,1,0:T(8,128)(2,1)S(1)}, bf16[1,256,5120]{2,1,0:T(8,128)(2,1)}, u32[]{:S(2)}) copy-start(bf16[1,256,5120]{2,1,0:T(8,128)(2,1)} %param.12) | copy-start | bytes 7864324

commit v2 on v0

v2 whole, which is shorter than its diff:
```python
import jax
import jax.numpy as jnp
from jax import lax
from jax.experimental import pallas as pl
from jax.experimental.pallas import tpu as pltpu
from jax.sharding import PartitionSpec as P

D = 5120
HD = 128
HW = 2560
ROWS = 256
COLS = 640
HEADS_HERE = 5
QUARTER = 160
EPS = 1e-06
MESH = pl.DeviceIdType.MESH
ANY = pl.BlockSpec(memory_space=pl.ANY)
VMEM = pl.BlockSpec(memory_space=pltpu.VMEM)
LIMIT = 62 * 1024 * 1024


def remote(src, dst, send, recv, device):
    return pltpu.make_async_remote_copy(
        src_ref=src, dst_ref=dst, send_sem=send, recv_sem=recv, device_id=device, device_id_type=MESH
    )


def place():
    x, s, tp = lax.axis_index("own"), lax.axis_index("seq"), lax.axis_index("tp")
    return x, s, tp


def greet(devices, extra=None):
    barrier = pltpu.get_barrier_semaphore()
    for device in devices:
        pl.semaphore_signal(barrier, inc=1, device_id=device, device_id_type=MESH)
    if extra is not None:
        extra(barrier)
    pl.semaphore_wait(barrier, len(devices))


def gather_sems(count):
    return [
        pltpu.SemaphoreType.DMA((36 * count,)),
        pltpu.SemaphoreType.DMA((20 * count,)),
        pltpu.SemaphoreType.DMA((16 * count,)),
    ]


def neighbours():
    x, s, tp = place()
    core, z, y = tp % 2, s // 2, (s % 2) * 2 + tp // 2

    def device(dx, dz, dy):
        y2 = (y + dy) % 4
        return ((x + dx) % 4, ((z + dz) % 4) * 2 + y2 // 2, (y2 % 2) * 2 + core)

    return [
        device(0, 1, 0), device(0, 3, 0), device(0, 0, 1), device(0, 0, 3),
        device(1, 0, 0), device(2, 0, 0), device(3, 0, 0), (x, s, tp + 1 - 2 * core),
    ]


class Gather:
    def __init__(self, own, slot, dest, half, send_sem, recv_sem, pair_sem, turn=0):
        self.x, s, tp = place()
        core, yl = tp % 2, tp // 2
        z, y = s // 2, (s % 2) * 2 + yl
        self.core, self.z, self.y = core, z, y
        self.own, self.slot, self.dest, self.half = own, slot, dest, half
        self.send_sem, self.recv_sem, self.pair_sem = send_sem, recv_sem, pair_sem
        self.sent = []
        self.base = (36 * turn, 20 * turn, 16 * turn)

        def device(dz, dy):
            z2, y2 = (z + dz) % 4, (y + dy) % 4
            return (self.x, z2 * 2 + y2 // 2, (y2 % 2) * 2 + core)

        self.first = {d: device((1 - core) * d, core * d) for d in (1, 3)}
        self.second = {d: device(core * d, (1 - core) * d) for d in (1, 3)}
        self.sibling = (self.x, s, tp + 1 - 2 * core)
        self.recv_index = {(1, 0): 0, (3, 0): 1, (2, 0): 2}
        for k in range(4):
            self.recv_index[(k, 1)] = 4 + 4 * k
            self.recv_index[(k, 3)] = 5 + 4 * k
            self.recv_index[(k, 2)] = 6 + 4 * k

    def push(self, src, dst, recv, device):
        copy = remote(src, dst, self.send_sem.at[self.base[0] + len(self.sent)], recv, device)
        copy.start()
        self.sent.append(copy)

    def to_sibling(self, k, j, src=None):
        src = self.slot(0, k, j) if src is None else src
        self.push(src, self.dest(1, k, j, k, j), self.pair_sem.at[self.base[2] + 4 * k + j], self.sibling)

    def along_second(self, k, src=None):
        src = self.slot(0, k, 0) if src is None else src
        for d in (1, 3):
            j = (0 - d) % 4
            self.push(src, self.dest(0, k, 0, k, j), self.recv_sem.at[self.base[1] + self.recv_index[(k, j)]], self.second[d])

    def begin(self):
        for d in (1, 3):
            k = (0 - d) % 4
            self.push(self.own, self.dest(0, 0, 0, k, 0), self.recv_sem.at[self.base[1] + self.recv_index[(k, 0)]], self.first[d])
        self.along_second(0, self.own)
        self.to_sibling(0, 0, self.own)

    def take(self, ref, sem):
        remote(ref, ref, self.send_sem.at[self.base[0]], sem, self.sibling).wait_recv()

    def first_near(self, k):
        self.take(self.slot(0, k, 0), self.recv_sem.at[self.base[1] + self.recv_index[(k, 0)]])
        h, d = (0, 1) if k == 3 else (1, 3)
        self.push(
            self.half(self.slot(0, k, 0), h), self.half(self.dest(0, k, 0, 2, 0), h),
            self.recv_sem.at[self.base[1] + self.recv_index[(2, 0)] + h], self.first[d],
        )
        self.along_second(k)
        self.to_sibling(k, 0)

    def first_far(self):
        for h in range(2):
            self.take(self.half(self.slot(0, 2, 0), h), self.recv_sem.at[self.base[1] + self.recv_index[(2, 0)] + h])
        self.along_second(2)
        self.to_sibling(2, 0)

    def second_near(self, k):
        for j in (3, 1):
            self.take(self.slot(0, k, j), self.recv_sem.at[self.base[1] + self.recv_index[(k, j)]])
            h, d = (0, 1) if j == 3 else (1, 3)
            self.push(
                self.half(self.slot(0, k, j), h), self.half(self.dest(0, k, j, k, 2), h),
                self.recv_sem.at[self.base[1] + self.recv_index[(k, 2)] + h], self.second[d],
            )
            self.to_sibling(k, j)

    def second_far(self, k):
        for h in range(2):
            self.take(self.half(self.slot(0, k, 2), h), self.recv_sem.at[self.base[1] + self.recv_index[(k, 2)] + h])
        self.to_sibling(k, 2)

    def from_sibling(self, k, j):
        self.take(self.slot(1, k, j), self.pair_sem.at[self.base[2] + 4 * k + j])

    def finish(self):
        for copy in self.sent:
            copy.wait_send()


ORDER = (1, 2, 0)


def qkv_kernel(root, w_ref, wo_ref, gain_ref, x_ref, mod_ref, q_out, kv_out, wo_out,
               wbuf, xbuf, xraw, acc, sums, gain, w_mid, wo_mid, gain_mid,
               send_sem, recv_sem, pair_sem, spread_send, spread_recv, mid_recv, mid_send, spread_local,
               x_send, x_recv, x_local, wo_send, wo_recv, sum_send, sum_recv):
    x, s, tp = place()
    core = tp % 2
    z, yh = s // 2, s % 2
    y = yh * 2 + tp // 2
    a0 = z * (1 - core) + y * core
    b0 = z * core + y * (1 - core)
    far = (root + 2) % 4
    mid = (root + 3) % 4 if ((far ^ 1) - root) % 4 == 1 else (root + 1) % 4

    turn_of = (x - tp) % 4

    raw = pltpu.make_async_copy(x_ref, xraw, x_local.at[4])

    @pl.when(turn_of == 0)
    def _():
        raw.start()

    barrier = pltpu.get_barrier_semaphore()
    near = neighbours() + [(x, s + 1 - 2 * yh, tp)]
    for device in near:
        pl.semaphore_signal(barrier, inc=1, device_id=device, device_id_type=MESH)
    for group in range(4):
        @pl.when(jnp.logical_not((x == root) & (tp == group)))
        def _(group=group):
            pl.semaphore_signal(barrier, inc=1, device_id=(root, s, group), device_id_type=MESH)

        @pl.when(jnp.logical_not((x == root) & (tp == group) & (z == tp)))
        def _(group=group):
            pl.semaphore_signal(barrier, inc=1, device_id=(root, tp * 2 + yh, group), device_id_type=MESH)

    greeted = jnp.where(x == root, jnp.where(z == tp, 30, 31), 0)
    pl.semaphore_wait(barrier, len(near) + greeted)

    def quarter_of(ref, j, quarter):
        return ref.at[j, pl.ds(quarter * QUARTER, QUARTER), :]

    def w_place(j, quarter):
        return wbuf.at[j, s, pl.ds(quarter * QUARTER, QUARTER), :]

    def wo_place(z2, yh2):
        return wo_out.at[pl.ds(pl.multiple_of(z2 * QUARTER, 32), QUARTER), pl.ds(pl.multiple_of(yh2 * COLS, 128), COLS)]

    def root_copies(group, act):
        plane = mid if group == far else group
        through = group == far
        sems = mid_recv if through else spread_recv
        for c, j in enumerate(ORDER):
            for quarter in range(4):
                piece = quarter_of(w_ref, j, quarter)
                land = w_mid.at[c] if through else w_place(j, quarter)
                if plane == root and quarter == group:
                    act(pltpu.make_async_copy(piece, land, spread_local.at[c]), True)
                else:
                    act(remote(piece, land, spread_send.at[4 * c + quarter], sems.at[c], (plane, s, quarter)), False)
                if c == 0:
                    land = gain_mid if through else gain
                    if plane == root and quarter == group:
                        act(pltpu.make_async_copy(gain_ref, land, spread_local.at[4]), True)
                    else:
                        act(remote(gain_ref, land, spread_send.at[16 + quarter], sems.at[4], (plane, s, quarter)), False)
        for quarter in range(4):
            piece = wo_ref.at[pl.ds(quarter * QUARTER, QUARTER), :]
            land = wo_mid if through else wo_place(quarter, yh)

            def go(piece=piece, land=land, quarter=quarter):
                act(remote(piece, land, spread_send.at[12 + quarter], sems.at[3], (plane, quarter * 2 + yh, z)), False)

            if plane == root:
                here = (z == group) & (z == quarter)

                @pl.when(here)
                def _(piece=piece, land=land):
                    act(pltpu.make_async_copy(piece, land, spread_local.at[3]), True)

                pl.when(jnp.logical_not(here))(go)
            else:
                go()

    def start(copy, here):
        copy.start()

    def drain(copy, here):
        if not here:
            copy.wait_send()

    @pl.when(x == root)
    def _():
        for group in range(4):
            pl.when(tp == group)(lambda group=group: root_copies(group, start))

    def mid_copy(i):
        held = (w_mid.at[0], w_mid.at[1], w_mid.at[2], wo_mid, gain_mid)[i]
        if i < 3:
            land = wbuf.at[ORDER[i], s, pl.ds(pl.multiple_of(tp * QUARTER, 32), QUARTER), :]
        else:
            land = (wo_place(z, yh), gain)[i - 3]
        return remote(held, held, mid_send.at[i], mid_recv.at[i], (far, s, tp)), remote(
            held, land, mid_send.at[i], spread_recv.at[i], (far, s, tp)
        )

    def relay(i):
        @pl.when(x == mid)
        def _():
            arrived, hop = mid_copy(i)
            arrived.wait_recv()
            hop.start()

    def own_place(i):
        if i < 3:
            return wbuf.at[ORDER[i], s, pl.ds(pl.multiple_of(tp * QUARTER, 32), QUARTER), :]
        return (wo_place(z, yh), gain)[i - 3]

    def arrive(i):
        ref = own_place(i)
        here = (x == root) & (tp == root)
        if i == 3:
            here = here & (z == root)

        @pl.when(here)
        def _():
            pltpu.make_async_copy(ref, ref, spread_local.at[i]).wait()

        @pl.when(jnp.logical_not(here))
        def _():
            remote(ref, ref, spread_send.at[0], spread_recv.at[i], (x, s, tp)).wait_recv()

    def chunk(c):
        j = ORDER[c]

        def slot(pair, k, m):
            if pair:
                a, b, kind = (b0 + k) % 4, (a0 + m) % 4, 1 - core
            else:
                a, b, kind = (a0 + k) % 4, (b0 + m) % 4, core
            z2 = a * (1 - kind) + b * kind
            y2 = a * kind + b * (1 - kind)
            offset = pl.multiple_of(((y2 % 2) * 2 + kind) * QUARTER, 32)
            return wbuf.at[j, z2 * 2 + y2 // 2, pl.ds(offset, QUARTER), :]

        def dest(pair, k, m, k2, m2):
            return slot(0, k, m)

        def half(ref, h):
            return ref.at[pl.ds(h * (QUARTER // 2), QUARTER // 2), :]

        return Gather(slot(0, 0, 0), slot, dest, half, send_sem, recv_sem, pair_sem, c)

    parts = [chunk(c) for c in range(3)]

    rows = ROWS // 4
    part = [pl.ds(i * rows, rows) for i in range(4)]
    up, down = ((x + 1) % 4, s, tp), ((x + 3) % 4, s, tp)
    forward = turn_of == 3 - 2 * core
    onward = ((x + 3 + 2 * core) % 4, s, tp)

    def x_copy(i, n, device):
        return remote(xbuf.at[part[i]], xbuf.at[part[i]], x_send.at[4 * n + i], x_recv.at[i], device)

    def normalize():
        @pl.when(turn_of == 0)
        def _():
            raw.wait()
            shift, scale = mod_ref[0:1], 1.0 + mod_ref[1:2]

            def body(i, carry):
                at = pl.ds(pl.multiple_of(i * 16, 16), 16)
                inputs = xraw[at].astype(jnp.float32)
                center = jnp.mean(inputs, axis=-1, keepdims=True)
                spread = jnp.mean((inputs - center) ** 2, axis=-1, keepdims=True)
                normed = (inputs - center) * lax.rsqrt(spread + EPS)
                xbuf[at] = (normed * scale + shift).astype(jnp.bfloat16)
                return carry

            lax.fori_loop(0, ROWS // 16, body, 0)

    def send_tokens():
        @pl.when(turn_of == 0)
        def _():
            for i in range(4):
                x_copy(i, 0, up).start()
                x_copy(i, 1, down).start()

    def pass_tokens(i):
        @pl.when(forward)
        def _():
            x_copy(i, 0, onward).wait_recv()
            x_copy(i, 0, onward).start()

    def need_tokens():
        @pl.when((turn_of != 0) & jnp.logical_not(forward))
        def _():
            for i in range(4):
                x_copy(i, 0, up).wait_recv()

    def dots(c):
        j = ORDER[c]
        acc[j] = jnp.zeros((ROWS, COLS), jnp.float32)

        def body(row, carry):
            tokens = xbuf[:, pl.ds(pl.multiple_of(row * COLS, 128), COLS)]
            acc[j] += jnp.dot(tokens, wbuf[j, row], preferred_element_type=jnp.float32)
            return carry

        lax.fori_loop(0, 8, body, 0)

    def siblings(c):
        for k in range(4):
            for m in range(4):
                parts[c].from_sibling(k, m)

    def row_sum(j):
        return jnp.broadcast_to(jnp.sum(acc[j] * acc[j], axis=1, keepdims=True), (ROWS, 128))

    def share(n):
        return [
            remote(sums.at[n, 0], sums.at[n, d], sum_send.at[4 * n + d], sum_recv.at[4 * n + d], ((x + d) % 4, s, tp))
            for d in (1, 2, 3)
        ]

    def scale_of(n):
        total = (sums[n, 0] + sums[n, 1]) + (sums[n, 2] + sums[n, 3])
        return lax.rsqrt(total / HW + EPS)[:, 0:1]

    normalize()
    relay(4)
    relay(0)
    arrive(4)
    arrive(0)
    g = parts[0]
    g.begin()
    send_tokens()
    g.first_near(3)
    g.first_near(1)
    g.second_near(0)
    g.first_far()
    relay(1)
    g.second_near(3)
    g.second_near(1)
    g.second_near(2)
    arrive(1)
    before = g
    for c in (1, 2):
        g = parts[c]
        g.begin()
        for k in (0, 3, 1, 2):
            before.second_far(k)
        g.first_near(3)
        g.first_near(1)
        g.second_near(0)
        g.first_far()
        pass_tokens(2 * c - 2)
        if c == 1:
            relay(2)
        g.second_near(3)
        g.second_near(1)
        g.second_near(2)
        pass_tokens(2 * c - 1)
        if c == 1:
            arrive(2)
        before = g

    partner = (x, s + 1 - 2 * yh, tp)
    z_up, z_down = (x, ((z + 1) % 4) * 2 + yh, tp), (x, ((z + 3) % 4) * 2 + yh, tp)
    other = 1 - yh

    def wo_copy(i, z2, yh2, device):
        return remote(wo_place(z2, yh2), wo_place(z2, yh2), wo_send.at[i], wo_recv.at[i], device)

    z_prev, z_next, z_far = (z + 3) % 4, (z + 1) % 4, (z + 2) % 4
    relay(3)
    arrive(3)
    wo_steps = [wo_copy(0, z, yh, partner), wo_copy(1, z, yh, z_up), wo_copy(2, z, yh, z_down)]
    for copy in wo_steps:
        copy.start()

    siblings(0)
    need_tokens()
    dots(0)
    sums[0, 0] = row_sum(1)
    siblings(1)
    key_shares = share(0)
    for copy in key_shares:
        copy.start()

    def wo_more(copy):
        copy.start()
        wo_steps.append(copy)

    wo_copy(0, z, other, partner).wait_recv()
    wo_more(wo_copy(3, z, other, z_up))
    wo_more(wo_copy(4, z, other, z_down))
    dots(1)
    kv_out[:, COLS:] = acc[2].astype(jnp.bfloat16)
    wo_copy(1, z_prev, yh, partner).wait_recv()
    wo_more(wo_copy(5, z_prev, yh, z_up))
    for copy in key_shares:
        copy.wait()
    gains = gain[...].astype(jnp.float32)
    kv_out[:, :COLS] = (acc[1] * scale_of(0) * gains[1:2]).astype(jnp.bfloat16)
    for k in (0, 3, 1, 2):
        before.second_far(k)
    wo_copy(4, z_next, other, partner).wait_recv()
    wo_more(wo_copy(6, z_next, other, z_down))
    siblings(2)
    dots(2)
    sums[1, 0] = row_sum(0)
    wo_copy(2, z_next, yh, partner).wait_recv()
    wo_copy(3, z_prev, other, partner).wait_recv()
    query_shares = share(1)
    for copy in query_shares:
        copy.start()
    for gather in parts:
        gather.finish()

    @pl.when(x == root)
    def _():
        for group in range(4):
            pl.when(tp == group)(lambda group=group: root_copies(group, drain))

    @pl.when(x == mid)
    def _():
        for i in range(5):
            mid_copy(i)[1].wait_send()

    @pl.when(turn_of == 0)
    def _():
        for i in range(4):
            x_copy(i, 0, up).wait_send()
            x_copy(i, 1, down).wait_send()

    @pl.when(forward)
    def _():
        for i in range(4):
            x_copy(i, 0, onward).wait_send()

    for copy in query_shares:
        copy.wait()
    q_out[...] = (acc[0] * scale_of(1) * gains[0:1]).astype(jnp.bfloat16)
    wo_copy(5, z_far, yh, partner).wait_recv()
    wo_copy(6, z_far, other, partner).wait_recv()
    for copy in wo_steps:
        copy.wait_send()


def qkv_call(root, w, wo, gain, x, mod):
    return pl.pallas_call(
        lambda *refs: qkv_kernel(root, *refs),
        out_shape=[
            jax.ShapeDtypeStruct((ROWS, COLS), jnp.bfloat16),
            jax.ShapeDtypeStruct((ROWS, 2 * COLS), jnp.bfloat16),
            jax.ShapeDtypeStruct((COLS, 2 * COLS), jnp.bfloat16),
        ],
        in_specs=[ANY, ANY, ANY, ANY, VMEM],
        out_specs=[VMEM, VMEM, ANY],
        scratch_shapes=[
            pltpu.VMEM((3, 8, COLS, COLS), jnp.bfloat16),
            pltpu.VMEM((ROWS, D), jnp.bfloat16),
            pltpu.VMEM((ROWS, D), jnp.bfloat16),
            pltpu.VMEM((3, ROWS, COLS), jnp.float32),
            pltpu.VMEM((2, 4, ROWS, 128), jnp.float32),
            pltpu.VMEM((16, COLS), jnp.bfloat16),
            pltpu.VMEM((3, QUARTER, COLS), jnp.bfloat16),
            pltpu.VMEM((QUARTER, COLS), jnp.bfloat16),
            pltpu.VMEM((16, COLS), jnp.bfloat16),
            *gather_sems(3),
            pltpu.SemaphoreType.DMA((20,)),
            pltpu.SemaphoreType.DMA((5,)),
            pltpu.SemaphoreType.DMA((5,)),
            pltpu.SemaphoreType.DMA((5,)),
            pltpu.SemaphoreType.DMA((5,)),
            pltpu.SemaphoreType.DMA((8,)),
            pltpu.SemaphoreType.DMA((4,)),
            pltpu.SemaphoreType.DMA((5,)),
            pltpu.SemaphoreType.DMA((7,)),
            pltpu.SemaphoreType.DMA((7,)),
            pltpu.SemaphoreType.DMA((8,)),
            pltpu.SemaphoreType.DMA((8,)),
        ],
        compiler_params=pltpu.CompilerParams(has_side_effects=True, vmem_limit_bytes=LIMIT, collective_id=1 + root),
        name=f"qkv_{root}",
    )(w, wo, gain, x, mod)


def attend_kernel(q_ref, kv_ref, wo_ref, x_ref, policy_ref, mod_ref, block_out, err_out,
                  inputs_ref, gate_ref, kvbuf, wofull, acc, top, low, attn, pair_attn, afull, proj, errs,
                  send_sem, recv_sem, pair_sem, wo_send, wo_recv, local_sem,
                  a_send, a_recv, a_pair_send, a_pair_recv, y_send, y_recv, e_send, e_recv):
    x, s, tp = place()
    core = tp % 2
    share_cols = pl.ds(pl.multiple_of(tp * (D // 4), 128), D // 4)
    own_inputs = pltpu.make_async_copy(x_ref.at[:, share_cols], inputs_ref, local_sem.at[6])
    own_gate = pltpu.make_async_copy(mod_ref.at[:, share_cols], gate_ref, local_sem.at[7])
    own_inputs.start()
    own_gate.start()
    greet(neighbours() + [(x, s, 3 - tp)])

    def slot(pair, k, j):
        return kvbuf.at[pair, 4 * k + j]

    def dest(pair, k, j, k2, j2):
        return kvbuf.at[pair, 4 * k2 + j2]

    def half(ref, h):
        return ref.at[pl.ds(h * (ROWS // 2), ROWS // 2), :]

    gather = Gather(kv_ref, slot, dest, half, send_sem, recv_sem, pair_sem)
    gather.begin()
    own_kv = pltpu.make_async_copy(kv_ref, slot(0, 0, 0), local_sem.at[0])
    own_kv.start()

    up, down = ((x + 1) % 4, s, tp), ((x + 3) % 4, s, tp)
    rows = [pl.ds(0, COLS // 2), pl.ds(COLS // 2, COLS // 2)]

    def wo_copy(i, src, plane, h, device, n):
        return remote(src, wofull.at[plane, rows[h]], wo_send.at[i], wo_recv.at[n], device)

    own_sends = [
        wo_copy(0, wo_ref.at[rows[0]], x, 0, up, 0),
        wo_copy(1, wo_ref.at[rows[1]], x, 1, down, 1),
        wo_copy(2, wo_ref.at[rows[1]], x, 1, up, 2),
        wo_copy(3, wo_ref.at[rows[0]], x, 0, down, 3),
    ]
    for copy in own_sends:
        copy.start()
    own_wo = pltpu.make_async_copy(wo_ref, wofull.at[x], local_sem.at[1])
    own_wo.start()
    below, above, across = (x + 3) % 4, (x + 1) % 4, (x + 2) % 4
    onward = [
        wo_copy(4, wofull.at[below, rows[0]], below, 0, up, 4),
        wo_copy(5, wofull.at[above, rows[1]], above, 1, down, 5),
    ]

    def pass_wo():
        wo_copy(4, wofull.at[below, rows[0]], below, 0, up, 0).wait_recv()
        onward[0].start()
        wo_copy(5, wofull.at[above, rows[1]], above, 1, down, 1).wait_recv()
        onward[1].start()

    def need_wo():
        own_wo.wait()
        wo_copy(2, wo_ref.at[rows[1]], below, 1, up, 2).wait_recv()
        wo_copy(3, wo_ref.at[rows[0]], above, 0, up, 3).wait_recv()
        wo_copy(4, wo_ref.at[rows[0]], across, 0, up, 4).wait_recv()
        wo_copy(5, wo_ref.at[rows[1]], across, 1, up, 5).wait_recv()

    acc[...] = jnp.zeros_like(acc)
    low[...] = jnp.zeros_like(low)
    top[...] = jnp.full_like(top, -1e30)
    factor = float(HD) ** -0.5 * 1.4426950408889634

    def step(h, pair, k):
        cols = pl.ds(pl.multiple_of(h * HD, HD), HD)
        vcols = pl.ds(pl.multiple_of(COLS + h * HD, HD), HD)
        keys = kvbuf[pair, pl.ds(4 * k, 4), :, cols].reshape(4 * ROWS, HD)
        values = kvbuf[pair, pl.ds(4 * k, 4), :, vcols].reshape(4 * ROWS, HD)
        scores = lax.dot_general(
            q_ref[:, cols], keys, (((1,), (1,)), ((), ())), preferred_element_type=jnp.float32
        )
        old = top[h]
        new = jnp.maximum(old, jnp.max(scores, axis=1, keepdims=True))
        top[h] = new
        decay = jnp.exp2((old - new) * factor)
        probs = jnp.exp2((scores - new[:, 0:1]) * factor)
        part = probs[:, 0:128]
        for i in range(1, 4 * ROWS // 128):
            part = part + probs[:, i * 128 : (i + 1) * 128]
        low[h] = low[h] * decay + part
        acc[h] = acc[h] * decay + jnp.dot(probs.astype(jnp.bfloat16), values, preferred_element_type=jnp.float32)

    def flash(pair, k):
        def body(h, carry):
            step(h, pair, k)
            return carry

        lax.fori_loop(0, HEADS_HERE, body, 0)

    def siblings(k):
        for j in range(4):
            gather.from_sibling(k, j)

    gather.first_near(3)
    gather.first_near(1)
    gather.second_near(0)
    gather.first_far()
    gather.second_near(3)
    pass_wo()
    own_kv.wait()
    gather.second_far(0)
    flash(0, 0)
    gather.second_near(1)
    gather.second_far(3)
    siblings(0)
    flash(1, 0)
    flash(0, 3)
    gather.second_near(2)
    gather.second_far(1)
    siblings(3)
    flash(1, 3)
    flash(0, 1)
    gather.second_far(2)
    siblings(1)
    flash(1, 1)
    siblings(2)

    partner = (tp + 2) % 4
    sibling = (x, s, tp + 1 - 2 * core)
    mine = x % 2 == core
    spans = [pl.ds(0, 3 * HD), pl.ds(3 * HD, 2 * HD)]

    def swap(g):
        return remote(attn.at[:, spans[g]], pair_attn.at[:, spans[g]], y_send.at[g], y_recv.at[g], (x, s, partner))

    def near(i, g):
        held = (attn, pair_attn)[i]
        return pltpu.make_async_copy(held.at[:, spans[g]], afull.at[x, :, spans[g]], local_sem.at[2 + 2 * i + g])

    def away(i, g, plane):
        held = (attn, pair_attn)[i]
        return remote(
            held.at[:, spans[g]], afull.at[plane, :, spans[g]], a_send.at[2 * i + g], a_recv.at[2 * plane + g],
            ((tp, partner)[i], s, tp),
        )

    def deliver(i, g):
        block = (tp, partner)[i]

        @pl.when(x == block)
        def _():
            near(i, g).start()

        @pl.when(x != block)
        def _():
            away(i, g, x).start()

    def pair_copy(g, d):
        ref = afull.at[(x + d) % 4, :, spans[g]]
        return remote(ref, ref, a_pair_send.at[4 * g + d], a_pair_recv.at[4 * g + d], sibling)

    def collect(g, d):
        @pl.when(mine)
        def _():
            if d == 0:
                @pl.when(x == tp)
                def _():
                    near(0, g).wait()

                @pl.when(x != tp)
                def _():
                    near(1, g).wait()
            else:
                away(0, g, (x + d) % 4).wait_recv()
            pair_copy(g, d).start()

        @pl.when(jnp.logical_not(mine))
        def _():
            pair_copy(g, d).wait_recv()

    def last(h, carry):
        step(h, 0, 2)
        step(h, 1, 2)
        total = jnp.sum(low[h], axis=1, keepdims=True)
        attn[:, pl.ds(pl.multiple_of(h * HD, HD), HD)] = (acc[h] / total).astype(jnp.bfloat16)

        @pl.when(h == 3)
        def _():
            swap(0).start()
            deliver(0, 0)

        return carry

    lax.fori_loop(0, HEADS_HERE, last, 0)
    need_wo()
    swap(1).start()
    deliver(0, 1)
    swap(0).wait_recv()
    deliver(1, 0)

    def project(g, d):
        plane = (x + d) % 4
        first, count = ((0, 3 * HD), (3 * HD, 2 * HD))[g]
        return jnp.dot(
            afull[plane, :, first : first + count], wofull[plane, first : first + count, :],
            preferred_element_type=jnp.float32,
        )

    swap(1).wait_recv()
    deliver(1, 1)
    for d in (0, 1, 3, 2):
        collect(0, d)
        if d == 0:
            proj[...] = project(0, d)
        else:
            proj[...] += project(0, d)
    for d in (0, 1, 3, 2):
        collect(1, d)
        proj[...] += project(1, d)

    own_inputs.wait()
    own_gate.wait()
    block = (inputs_ref[...].astype(jnp.float32) + gate_ref[2:3] * proj[...]).astype(jnp.bfloat16)
    block_out[...] = block
    differ = block.astype(jnp.float32) - policy_ref[...].astype(jnp.float32)
    errs[0] = jnp.broadcast_to(jnp.sum(differ * differ, axis=1, keepdims=True), (ROWS, 128))
    for i in range(2):
        for g in range(2):
            @pl.when(x != (tp, partner)[i])
            def _(i=i, g=g):
                away(i, g, x).wait_send()
    for g in range(2):
        swap(g).wait_send()

    @pl.when(mine)
    def _():
        for g in range(2):
            for d in range(4):
                pair_copy(g, d).wait_send()

    shares = [remote(errs.at[0], errs.at[d], e_send.at[d], e_recv.at[d], (x, s, (tp + d) % 4)) for d in (1, 2, 3)]
    for share in shares:
        share.start()
    for copy in own_sends + onward:
        copy.wait_send()
    gather.finish()
    for share in shares:
        share.wait()
    err_out[...] = ((errs[0] + errs[1]) + (errs[2] + errs[3])) / D


def attend_call(q, kv, wo, x, policy, mod):
    return pl.pallas_call(
        attend_kernel,
        out_shape=[
            jax.ShapeDtypeStruct((ROWS, D // 4), jnp.bfloat16),
            jax.ShapeDtypeStruct((ROWS, 128), jnp.float32),
        ],
        in_specs=[VMEM, ANY, ANY, ANY, VMEM, ANY],
        out_specs=[VMEM, VMEM],
        scratch_shapes=[
            pltpu.VMEM((ROWS, D // 4), jnp.bfloat16),
            pltpu.VMEM((8, D // 4), jnp.float32),
            pltpu.VMEM((2, 16, ROWS, 2 * COLS), jnp.bfloat16),
            pltpu.VMEM((4, COLS, 2 * COLS), jnp.bfloat16),
            pltpu.VMEM((HEADS_HERE, ROWS, HD), jnp.float32),
            pltpu.VMEM((HEADS_HERE, ROWS, HD), jnp.float32),
            pltpu.VMEM((HEADS_HERE, ROWS, HD), jnp.float32),
            pltpu.VMEM((ROWS, COLS), jnp.bfloat16),
            pltpu.VMEM((ROWS, COLS), jnp.bfloat16),
            pltpu.VMEM((4, ROWS, COLS), jnp.bfloat16),
            pltpu.VMEM((ROWS, D // 4), jnp.float32),
            pltpu.VMEM((4, ROWS, 128), jnp.float32),
            *gather_sems(1),
            pltpu.SemaphoreType.DMA((6,)),
            pltpu.SemaphoreType.DMA((6,)),
            pltpu.SemaphoreType.DMA((8,)),
            pltpu.SemaphoreType.DMA((4,)),
            pltpu.SemaphoreType.DMA((8,)),
            pltpu.SemaphoreType.DMA((8,)),
            pltpu.SemaphoreType.DMA((8,)),
            pltpu.SemaphoreType.DMA((2,)),
            pltpu.SemaphoreType.DMA((2,)),
            pltpu.SemaphoreType.DMA((4,)),
            pltpu.SemaphoreType.DMA((4,)),
        ],
        compiler_params=pltpu.CompilerParams(has_side_effects=True, vmem_limit_bytes=LIMIT, collective_id=5),
        name="attend",
    )(q, kv, wo, x, policy, mod)


def local(latents, policy_out, w_qkv, w_out, qk_gains, mod_table, timestep, owner):
    held = w_qkv.shape[0]
    local_block = owner[0] % held
    root_group = owner[0] // held
    mine_qkv = lax.dynamic_index_in_dim(w_qkv.transpose(0, 2, 1, 3), local_block, 0, keepdims=False)
    mine_out = lax.dynamic_index_in_dim(w_out, local_block, 0, keepdims=False)
    mine_gains = lax.dynamic_index_in_dim(qk_gains, local_block, 0, keepdims=False)
    mine_gains = jnp.pad(mine_gains, ((0, 14), (0, 0)))
    onehot = (jnp.arange(mod_table.shape[0], dtype=jnp.int32) == timestep[0]).astype(jnp.float32)
    modulation = jnp.tensordot(onehot, mod_table, axes=1, precision=lax.Precision.HIGHEST)
    mod = jnp.pad(modulation, ((0, 5), (0, 0)))
    q, kv, wo_rows = lax.switch(
        root_group,
        [lambda *a, root=root: tuple(qkv_call(root, *a)) for root in range(4)],
        mine_qkv, mine_out, mine_gains, latents[0], mod,
    )
    block, squares = attend_call(q, kv, wo_rows, latents[0], policy_out[0], mod)
    return (block[None], squares[:, 0][None])


def solution(mesh):
    placed = (
        P(None, ("own", "seq"), None),
        P(None, ("own", "seq"), "tp"),
        P("own", "seq", None, "tp"),
        P("own", "tp", "seq"),
        P("own", None, "tp"),
        P(),
        P(),
        P(),
    )
    return jax.shard_map(
        local,
        mesh=mesh,
        in_specs=placed,
        out_specs=(P(None, ("own", "seq"), "tp"), P(None, ("own", "seq"))),
        check_vma=False,
    )
```

time: 716 us -> 253 us (0.35)
  waiting for transfers between devices: 573 us -> 0 us
  Pallas kernels: 0 us -> 239 us
  matrix products: 57 us -> 0.34 us
  other arithmetic: 33 us -> 0 us
  blocking collectives: 18.3 us -> 0 us
  between operations: 15.6 us -> 2.07 us
  local copies, waits for them, and re-layouts: 17.1 us -> 8.87 us
    all_gather x4 -> x0, waiting for transfers between devices: 464 us -> none  [the longest x1 200 us: local(): piece = lax.all_gather(weights_qkv, 'seq', axis=0, tiled=True)]
    pallas_call x0 -> x2, Pallas kernels: none -> 239 us  [the longest x1 134 us: qkv_call(): pl.pallas_call(lambda *refs: qkv_kernel(root, *refs), out_shape=[jax.Shap...]
    psum x1 -> x0, waiting for transfers between devices: 80.9 us -> none  [spread_2(): return lax.psum(kept, axis)]
    dot_general x4 -> x0, matrix products: 56.6 us -> none  [the longest x1 20 us: local(): jnp.einsum('hqk,khd->hqd', probs.astype(jnp.bfloat16), value_piece, prefe...]
    reduce_scatter x1 -> x0, waiting for transfers between devices: 28.4 us -> none  [local(): lax.psum_scatter(proj.astype(jnp.bfloat16), 'tp', scatter_dimension=1, ti...]
    reduce_sum x5 -> x0, other arithmetic: 22.8 us -> none  [the longest x1 17.5 us: local(): new_sum = jnp.sum(probs, axis=-1)]
    psum x3 -> x0, blocking collectives: 18.3 us -> none  [the longest x1 6.58 us: spread_2(): return lax.psum(kept, axis)]
  transfers between devices with their start and end apart: 6 -> 0, of which waited for: 6 -> 0; matrix products, arithmetic and copies ran while one was open for 9% -> 0% of each run, Pallas kernels for 0% -> 0%
where the time goes in v2:
time: 253 us; the launch traced here: 250 us
  Pallas kernels  239 us (94%)
  local copies, waits for them, and re-layouts  8.87 us (4%)
    pallas_call x1, Pallas kernels, qkv_call(): pl.pallas_call(lambda *refs: qkv_kernel(root, *refs), out_shape=[jax.Shap...  134 us
    pallas_call x1, Pallas kernels, attend_call(): pl.pallas_call(attend_kernel, out_shape=[jax.ShapeDtypeStruct((ROWS, D //...  105 us

profile of v2, /device:TPU:1, one launch (start us, length us, event | category | flops | bytes accessed | tf_op | source)
XLA Modules:
  0.0 250.4 jit_solution(2237917335768847441)
XLA Ops:
  0.6 0.0 copy-start
  2.0 0.7 dynamic-slice_bitcast_fusion.2
  2.7 0.0 copy-done
  2.7 0.3 fusion
  3.1 1.2 dynamic-slice_bitcast_fusion.1
  4.4 3.3 %dynamic-slice_bitcast_fusion = bf16[3,640,640]{2,1,0:T(8,128)(2,1)} fusion(bf16[4,640,3,640]{3,1,2,0:T(8,128)(2,1)} %param.14, s32[]{:T(128)S(6)} %select_n.21), kind=kLoop, calls=%fused_computation | loop fusion | bytes 4915204 | tf_op jit(solution)/shard_map/jit(dynamic_index_in_dim)/squeeze | solution.py:831
  7.7 134.0 %conditional.1 = ((bf16[256,640]{1,0:T(8,128)(2,1)S(1)}, bf16[256,1280]{1,0:T(8,128)(2,1)}, bf16[640,1280]{1,0:T(8,128)(2,1)})) conditional(s32[]{:T(128)} %clamp.3, (bf16[3,640,640]{2,1,0:T(8,128)(2,1)}, bf16[640,640]{1,0:T(8,128)(2,1)S(1)}, bf16[16,640]{1,0:T(8,128)(2,1)S(1)}, bf16[256,5120]{1,0:T(8,128)(2,1)}, ...), branch_computations={%region_0.1_spmd, %region_1.2_spmd, %region_2.3_spmd, %region_3.4_... | conditional | bytes 8 | solution.py:838
  7.7 133.8 %qkv_1.1 = (bf16[256,640]{1,0:T(8,128)(2,1)S(1)}, bf16[256,1280]{1,0:T(8,128)(2,1)}, bf16[640,1280]{1,0:T(8,128)(2,1)}) custom-call(bf16[3,640,640]{2,1,0:T(8,128)(2,1)} %get-tuple-element.45.refs_0_, bf16[640,640]{1,0:T(8,128)(2,1)S(1)} %get-tuple-element.46.refs_1_, bf16[16,640]{1,0:T(8,128)(2,1)S(1)} %get-tuple-element.47.refs_2_, ...), custom_call_target="tpu_custom_call" | custom-call | tf_op jit(solution)/shard_map/cond/branch_1_fun/qkv_1/pallas_call | solution.py:504
  141.8 105.1 %attend.1 = (bf16[256,1280]{1,0:T(8,128)(2,1)}, f32[256,128]{1,0:T(8,128)}) custom-call(bf16[256,640]{1,0:T(8,128)(2,1)S(1)} %get-tuple-element.67.q_ref, bf16[256,1280]{1,0:T(8,128)(2,1)} %get-tuple-element.68.kv_ref, bf16[640,1280]{1,0:T(8,128)(2,1)} %get-tuple-element.69.wo_ref, bf16[256,5120]{1,0:T(8,128)(2,1)} %bitcast.30, bf16[256,1280]{1,0:T(8,128)(2,1)} %bitcast.31, ...), custom_call_target="tpu_custom_call" | custom-call | tf_op jit(solution)/shard_map/attend/pallas_call | solution.py:788
  246.9 1.6 slice_reduce_fusion
  248.5 2.0 copy.28
  (3 shorter events, 0.0 us)
Async XLA Ops:
  0.6 2.1 copy-start

commit v3 on v2

--- a/solution.py
+++ b/solution.py
@@ -37,6 +37,14 @@
     if extra is not None:
         extra(barrier)
     pl.semaphore_wait(barrier, len(devices))
+
+
+def to_row(column):
+    return jnp.transpose(jnp.broadcast_to(column, (ROWS, 128)))[0:8]
+
+
+def to_column(row):
+    return jnp.transpose(jnp.broadcast_to(row[0:1], (128, ROWS)))[:, 0:1]
 
 
 def gather_sems(count):
@@ -367,7 +375,7 @@
                 parts[c].from_sibling(k, m)
 
     def row_sum(j):
-        return jnp.broadcast_to(jnp.sum(acc[j] * acc[j], axis=1, keepdims=True), (ROWS, 128))
+        return to_row(jnp.sum(acc[j] * acc[j], axis=1, keepdims=True))
 
     def share(n):
         return [
@@ -377,45 +385,55 @@
 
     def scale_of(n):
         total = (sums[n, 0] + sums[n, 1]) + (sums[n, 2] + sums[n, 3])
-        return lax.rsqrt(total / HW + EPS)[:, 0:1]
+        return to_column(lax.rsqrt(total / HW + EPS))
 
     normalize()
     relay(4)
     relay(0)
     arrive(4)
     arrive(0)
-    g = parts[0]
-    g.begin()
+    g0, g1, g2 = parts
+    g0.begin()
     send_tokens()
-    g.first_near(3)
-    g.first_near(1)
-    g.second_near(0)
-    g.first_far()
+    g0.first_near(3)
+    g0.first_near(1)
+    g0.second_near(0)
+    g0.first_far()
     relay(1)
-    g.second_near(3)
-    g.second_near(1)
-    g.second_near(2)
+    g0.second_near(3)
     arrive(1)
-    before = g
-    for c in (1, 2):
-        g = parts[c]
-        g.begin()
-        for k in (0, 3, 1, 2):
-            before.second_far(k)
-        g.first_near(3)
-        g.first_near(1)
-        g.second_near(0)
-        g.first_far()
-        pass_tokens(2 * c - 2)
-        if c == 1:
-            relay(2)
-        g.second_near(3)
-        g.second_near(1)
-        g.second_near(2)
-        pass_tokens(2 * c - 1)
-        if c == 1:
-            arrive(2)
-        before = g
+    g1.begin()
+    g0.second_near(1)
+    g1.first_near(3)
+    g1.first_near(1)
+    g0.second_near(2)
+    g1.second_near(0)
+    g1.first_far()
+    relay(2)
+    for k in (0, 3, 1, 2):
+        g0.second_far(k)
+    pass_tokens(0)
+    g1.second_near(3)
+    arrive(2)
+    g2.begin()
+    g1.second_near(1)
+    g2.first_near(3)
+    g2.first_near(1)
+    pass_tokens(1)
+    g1.second_near(2)
+    g2.second_near(0)
+    g2.first_far()
+    for k in (0, 3, 1, 2):
+        g1.second_far(k)
+    g2.second_near(3)
+    pass_tokens(2)
+    g2.second_near(1)
+    pass_tokens(3)
+    siblings(0)
+    need_tokens()
+    dots(0)
+    sums[0, 0] = row_sum(1)
+    g2.second_near(2)
 
     partner = (x, s + 1 - 2 * yh, tp)
     z_up, z_down = (x, ((z + 1) % 4) * 2 + yh, tp), (x, ((z + 3) % 4) * 2 + yh, tp)
@@ -431,10 +449,6 @@
     for copy in wo_steps:
         copy.start()
 
-    siblings(0)
-    need_tokens()
-    dots(0)
-    sums[0, 0] = row_sum(1)
     siblings(1)
     key_shares = share(0)
     for copy in key_shares:
@@ -456,7 +470,7 @@
     gains = gain[...].astype(jnp.float32)
     kv_out[:, :COLS] = (acc[1] * scale_of(0) * gains[1:2]).astype(jnp.bfloat16)
     for k in (0, 3, 1, 2):
-        before.second_far(k)
+        g2.second_far(k)
     wo_copy(4, z_next, other, partner).wait_recv()
     wo_more(wo_copy(6, z_next, other, z_down))
     siblings(2)
@@ -515,7 +529,7 @@
             pltpu.VMEM((ROWS, D), jnp.bfloat16),
             pltpu.VMEM((ROWS, D), jnp.bfloat16),
             pltpu.VMEM((3, ROWS, COLS), jnp.float32),
-            pltpu.VMEM((2, 4, ROWS, 128), jnp.float32),
+            pltpu.VMEM((2, 4, 8, ROWS), jnp.float32),
             pltpu.VMEM((16, COLS), jnp.bfloat16),
             pltpu.VMEM((3, QUARTER, COLS), jnp.bfloat16),
             pltpu.VMEM((QUARTER, COLS), jnp.bfloat16),
@@ -539,6 +553,18 @@
     )(w, wo, gain, x, mod)
 
 
+ARRIVAL = [
+    (0, 0, 0), (0, 3, 0), (0, 1, 0), (1, 0, 0),
+    (0, 0, 3), (0, 0, 1), (1, 3, 0), (1, 1, 0),
+    (0, 2, 0), (0, 3, 3), (0, 3, 1), (1, 0, 3),
+    (1, 0, 1), (1, 2, 0), (1, 3, 3), (1, 3, 1),
+    (0, 0, 2), (0, 1, 3), (0, 1, 1), (1, 0, 2),
+    (1, 1, 3), (1, 1, 1), (0, 3, 2), (1, 3, 2),
+    (0, 2, 3), (0, 2, 1), (1, 2, 3), (1, 2, 1),
+    (0, 1, 2), (0, 2, 2), (1, 1, 2), (1, 2, 2),
+]
+
+
 def attend_kernel(q_ref, kv_ref, wo_ref, x_ref, policy_ref, mod_ref, block_out, err_out,
                   inputs_ref, gate_ref, kvbuf, wofull, acc, top, low, attn, pair_attn, afull, proj, errs,
                   send_sem, recv_sem, pair_sem, wo_send, wo_recv, local_sem,
@@ -553,10 +579,10 @@
     greet(neighbours() + [(x, s, 3 - tp)])
 
     def slot(pair, k, j):
-        return kvbuf.at[pair, 4 * k + j]
+        return kvbuf.at[ARRIVAL.index((pair, k, j))]
 
     def dest(pair, k, j, k2, j2):
-        return kvbuf.at[pair, 4 * k2 + j2]
+        return kvbuf.at[ARRIVAL.index((pair, k2, j2))]
 
     def half(ref, h):
         return ref.at[pl.ds(h * (ROWS // 2), ROWS // 2), :]
@@ -606,11 +632,11 @@
     top[...] = jnp.full_like(top, -1e30)
     factor = float(HD) ** -0.5 * 1.4426950408889634
 
-    def step(h, pair, k):
+    def step(h, block):
         cols = pl.ds(pl.multiple_of(h * HD, HD), HD)
         vcols = pl.ds(pl.multiple_of(COLS + h * HD, HD), HD)
-        keys = kvbuf[pair, pl.ds(4 * k, 4), :, cols].reshape(4 * ROWS, HD)
-        values = kvbuf[pair, pl.ds(4 * k, 4), :, vcols].reshape(4 * ROWS, HD)
+        keys = kvbuf[4 * block : 4 * block + 4, :, cols].reshape(4 * ROWS, HD)
+        values = kvbuf[4 * block : 4 * block + 4, :, vcols].reshape(4 * ROWS, HD)
         scores = lax.dot_general(
             q_ref[:, cols], keys, (((1,), (1,)), ((), ())), preferred_element_type=jnp.float32
         )
@@ -625,40 +651,40 @@
         low[h] = low[h] * decay + part
         acc[h] = acc[h] * decay + jnp.dot(probs.astype(jnp.bfloat16), values, preferred_element_type=jnp.float32)
 
-    def flash(pair, k):
+    def flash(block):
+        for pair, k, j in ARRIVAL[4 * block : 4 * block + 4]:
+            if pair:
+                gather.from_sibling(k, j)
+
         def body(h, carry):
-            step(h, pair, k)
+            step(h, block)
             return carry
 
         lax.fori_loop(0, HEADS_HERE, body, 0)
-
-    def siblings(k):
-        for j in range(4):
-            gather.from_sibling(k, j)
 
     gather.first_near(3)
     gather.first_near(1)
     gather.second_near(0)
     gather.first_far()
+    own_kv.wait()
+    flash(0)
     gather.second_near(3)
+    flash(1)
     pass_wo()
-    own_kv.wait()
+    gather.second_near(1)
+    flash(2)
     gather.second_far(0)
-    flash(0, 0)
-    gather.second_near(1)
+    flash(3)
+    flash(4)
+    gather.second_near(2)
     gather.second_far(3)
-    siblings(0)
-    flash(1, 0)
-    flash(0, 3)
-    gather.second_near(2)
+    flash(5)
+    flash(6)
     gather.second_far(1)
-    siblings(3)
-    flash(1, 3)
-    flash(0, 1)
     gather.second_far(2)
-    siblings(1)
-    flash(1, 1)
-    siblings(2)
+    for pair, k, j in ARRIVAL[28:]:
+        if pair:
+            gather.from_sibling(k, j)
 
     partner = (tp + 2) % 4
     sibling = (x, s, tp + 1 - 2 * core)
@@ -714,8 +740,7 @@
             pair_copy(g, d).wait_recv()
 
     def last(h, carry):
-        step(h, 0, 2)
-        step(h, 1, 2)
+        step(h, 7)
         total = jnp.sum(low[h], axis=1, keepdims=True)
         attn[:, pl.ds(pl.multiple_of(h * HD, HD), HD)] = (acc[h] / total).astype(jnp.bfloat16)
 
@@ -758,7 +783,7 @@
     block = (inputs_ref[...].astype(jnp.float32) + gate_ref[2:3] * proj[...]).astype(jnp.bfloat16)
     block_out[...] = block
     differ = block.astype(jnp.float32) - policy_ref[...].astype(jnp.float32)
-    errs[0] = jnp.broadcast_to(jnp.sum(differ * differ, axis=1, keepdims=True), (ROWS, 128))
+    errs[0] = to_row(jnp.sum(differ * differ, axis=1, keepdims=True))
     for i in range(2):
         for g in range(2):
             @pl.when(x != (tp, partner)[i])
@@ -789,14 +814,14 @@
         attend_kernel,
         out_shape=[
             jax.ShapeDtypeStruct((ROWS, D // 4), jnp.bfloat16),
-            jax.ShapeDtypeStruct((ROWS, 128), jnp.float32),
+            jax.ShapeDtypeStruct((8, ROWS), jnp.float32),
         ],
         in_specs=[VMEM, ANY, ANY, ANY, VMEM, ANY],
         out_specs=[VMEM, VMEM],
         scratch_shapes=[
             pltpu.VMEM((ROWS, D // 4), jnp.bfloat16),
             pltpu.VMEM((8, D // 4), jnp.float32),
-            pltpu.VMEM((2, 16, ROWS, 2 * COLS), jnp.bfloat16),
+            pltpu.VMEM((32, ROWS, 2 * COLS), jnp.bfloat16),
             pltpu.VMEM((4, COLS, 2 * COLS), jnp.bfloat16),
             pltpu.VMEM((HEADS_HERE, ROWS, HD), jnp.float32),
             pltpu.VMEM((HEADS_HERE, ROWS, HD), jnp.float32),
@@ -805,7 +830,7 @@
             pltpu.VMEM((ROWS, COLS), jnp.bfloat16),
             pltpu.VMEM((4, ROWS, COLS), jnp.bfloat16),
             pltpu.VMEM((ROWS, D // 4), jnp.float32),
-            pltpu.VMEM((4, ROWS, 128), jnp.float32),
+            pltpu.VMEM((4, 8, ROWS), jnp.float32),
             *gather_sems(1),
             pltpu.SemaphoreType.DMA((6,)),
             pltpu.SemaphoreType.DMA((6,)),
@@ -841,7 +866,7 @@
         mine_qkv, mine_out, mine_gains, latents[0], mod,
     )
     block, squares = attend_call(q, kv, wo_rows, latents[0], policy_out[0], mod)
-    return (block[None], squares[:, 0][None])
+    return (block[None], squares[0:1])
 
 
 def solution(mesh):

time: 253 us -> 231 us (0.913)
  Pallas kernels: 239 us -> 219 us
    pallas_call x1, Pallas kernels: 105 us -> 90.6 us  [attend_call(): pl.pallas_call(attend_kernel, out_shape=[jax.ShapeDtypeStruct((ROWS, D //...]
    pallas_call x1, Pallas kernels: 134 us -> 128 us  [qkv_call(): pl.pallas_call(lambda *refs: qkv_kernel(root, *refs), out_shape=[jax.Shap...]
where the time goes in v3:
time: 231 us; the launch traced here: 230 us
  Pallas kernels  219 us (95%)
  local copies, waits for them, and re-layouts  8.55 us (4%)
    pallas_call x1, Pallas kernels, qkv_call(): pl.pallas_call(lambda *refs: qkv_kernel(root, *refs), out_shape=[jax.Shap...  128 us
    pallas_call x1, Pallas kernels, attend_call(): pl.pallas_call(attend_kernel, out_shape=[jax.ShapeDtypeStruct((ROWS, D //...  90.6 us

profile of v3, /device:TPU:1, one launch (start us, length us, event | category | flops | bytes accessed | tf_op | source)
XLA Modules:
  0.0 230.2 jit_solution(18417388699339567939)
XLA Ops:
  0.6 0.0 copy-start
  2.0 0.7 dynamic-slice_bitcast_fusion.2
  2.7 0.0 copy-done
  2.7 0.3 fusion
  3.1 1.2 dynamic-slice_bitcast_fusion.1
  4.4 3.4 %dynamic-slice_bitcast_fusion = bf16[3,640,640]{2,1,0:T(8,128)(2,1)} fusion(bf16[4,640,3,640]{3,1,2,0:T(8,128)(2,1)} %param.14, s32[]{:T(128)S(6)} %select_n.21), kind=kLoop, calls=%fused_computation | loop fusion | bytes 4915204 | tf_op jit(solution)/shard_map/jit(dynamic_index_in_dim)/squeeze | solution.py:856
  7.7 128.6 %conditional.1 = ((bf16[256,640]{1,0:T(8,128)(2,1)S(1)}, bf16[256,1280]{1,0:T(8,128)(2,1)}, bf16[640,1280]{1,0:T(8,128)(2,1)})) conditional(s32[]{:T(128)} %clamp.3, (bf16[3,640,640]{2,1,0:T(8,128)(2,1)}, bf16[640,640]{1,0:T(8,128)(2,1)S(1)}, bf16[16,640]{1,0:T(8,128)(2,1)S(1)}, bf16[256,5120]{1,0:T(8,128)(2,1)}, ...), branch_computations={%region_0.1_spmd, %region_1.2_spmd, %region_2.3_spmd, %region_3.4_... | conditional | bytes 8 | solution.py:863
  7.7 128.4 %qkv_0.1 = (bf16[256,640]{1,0:T(8,128)(2,1)S(1)}, bf16[256,1280]{1,0:T(8,128)(2,1)}, bf16[640,1280]{1,0:T(8,128)(2,1)}) custom-call(bf16[3,640,640]{2,1,0:T(8,128)(2,1)} %get-tuple-element.40.refs_0_, bf16[640,640]{1,0:T(8,128)(2,1)S(1)} %get-tuple-element.41.refs_1_, bf16[16,640]{1,0:T(8,128)(2,1)S(1)} %get-tuple-element.42.refs_2_, ...), custom_call_target="tpu_custom_call" | custom-call | tf_op jit(solution)/shard_map/cond/branch_0_fun/qkv_0/pallas_call | solution.py:518
  136.4 90.6 %attend.1 = (bf16[256,1280]{1,0:T(8,128)(2,1)}, f32[8,256]{1,0:T(8,128)}) custom-call(bf16[256,640]{1,0:T(8,128)(2,1)S(1)} %get-tuple-element.67.q_ref, bf16[256,1280]{1,0:T(8,128)(2,1)} %get-tuple-element.68.kv_ref, bf16[640,1280]{1,0:T(8,128)(2,1)} %get-tuple-element.69.wo_ref, bf16[256,5120]{1,0:T(8,128)(2,1)} %bitcast.29, bf16[256,1280]{1,0:T(8,128)(2,1)} %bitcast.30, ...), custom_call_target="tpu_custom_call" | custom-call | tf_op jit(solution)/shard_map/attend/pallas_call | solution.py:813
  227.0 1.3 slice.3
  228.3 2.0 copy.28
  (3 shorter events, 0.0 us)
Async XLA Ops:
  0.6 2.1 copy-start

commit v4 on v3

--- a/solution.py
+++ b/solution.py
@@ -224,6 +224,11 @@
                         act(pltpu.make_async_copy(gain_ref, land, spread_local.at[4]), True)
                     else:
                         act(remote(gain_ref, land, spread_send.at[16 + quarter], sems.at[4], (plane, s, quarter)), False)
+
+    def root_wo(group, act):
+        plane = mid if group == far else group
+        through = group == far
+        sems = mid_recv if through else spread_recv
         for quarter in range(4):
             piece = wo_ref.at[pl.ds(quarter * QUARTER, QUARTER), :]
             land = wo_mid if through else wo_place(quarter, yh)
@@ -249,10 +254,13 @@
         if not here:
             copy.wait_send()
 
-    @pl.when(x == root)
-    def _():
-        for group in range(4):
-            pl.when(tp == group)(lambda group=group: root_copies(group, start))
+    def at_root(copies, act):
+        @pl.when(x == root)
+        def _():
+            for group in range(4):
+                pl.when(tp == group)(lambda group=group: copies(group, act))
+
+    at_root(root_copies, start)
 
     def mid_copy(i):
         held = (w_mid.at[0], w_mid.at[1], w_mid.at[2], wo_mid, gain_mid)[i]
@@ -313,14 +321,13 @@
 
     parts = [chunk(c) for c in range(3)]
 
-    rows = ROWS // 4
-    part = [pl.ds(i * rows, rows) for i in range(4)]
+    part = [pl.ds(i * D // 4, D // 4) for i in range(4)]
     up, down = ((x + 1) % 4, s, tp), ((x + 3) % 4, s, tp)
     forward = turn_of == 3 - 2 * core
     onward = ((x + 3 + 2 * core) % 4, s, tp)
 
     def x_copy(i, n, device):
-        return remote(xbuf.at[part[i]], xbuf.at[part[i]], x_send.at[4 * n + i], x_recv.at[i], device)
+        return remote(xbuf.at[:, part[i]], xbuf.at[:, part[i]], x_send.at[4 * n + i], x_recv.at[i], device)
 
     def normalize():
         @pl.when(turn_of == 0)
@@ -339,8 +346,8 @@
 
             lax.fori_loop(0, ROWS // 16, body, 0)
 
-    def send_tokens():
-        @pl.when(turn_of == 0)
+    def send_tokens(now):
+        @pl.when((turn_of == 0) & now)
         def _():
             for i in range(4):
                 x_copy(i, 0, up).start()
@@ -352,22 +359,20 @@
             x_copy(i, 0, onward).wait_recv()
             x_copy(i, 0, onward).start()
 
-    def need_tokens():
+    def need_tokens(i):
         @pl.when((turn_of != 0) & jnp.logical_not(forward))
         def _():
-            for i in range(4):
-                x_copy(i, 0, up).wait_recv()
-
-    def dots(c):
+            x_copy(i, 0, up).wait_recv()
+
+    def dots(c, first, stop):
         j = ORDER[c]
-        acc[j] = jnp.zeros((ROWS, COLS), jnp.float32)
 
         def body(row, carry):
             tokens = xbuf[:, pl.ds(pl.multiple_of(row * COLS, 128), COLS)]
             acc[j] += jnp.dot(tokens, wbuf[j, row], preferred_element_type=jnp.float32)
             return carry
 
-        lax.fori_loop(0, 8, body, 0)
+        lax.fori_loop(first, stop, body, 0)
 
     def siblings(c):
         for k in range(4):
@@ -388,16 +393,17 @@
         return to_column(lax.rsqrt(total / HW + EPS))
 
     normalize()
+    send_tokens(x != root)
     relay(4)
     relay(0)
     arrive(4)
     arrive(0)
     g0, g1, g2 = parts
     g0.begin()
-    send_tokens()
     g0.first_near(3)
     g0.first_near(1)
     g0.second_near(0)
+    send_tokens(x == root)
     g0.first_far()
     relay(1)
     g0.second_near(3)
@@ -406,34 +412,44 @@
     g0.second_near(1)
     g1.first_near(3)
     g1.first_near(1)
+    pass_tokens(0)
     g0.second_near(2)
     g1.second_near(0)
     g1.first_far()
     relay(2)
     for k in (0, 3, 1, 2):
         g0.second_far(k)
-    pass_tokens(0)
+    pass_tokens(1)
     g1.second_near(3)
     arrive(2)
     g2.begin()
     g1.second_near(1)
     g2.first_near(3)
     g2.first_near(1)
-    pass_tokens(1)
+    pass_tokens(2)
     g1.second_near(2)
+    at_root(root_wo, start)
     g2.second_near(0)
     g2.first_far()
     for k in (0, 3, 1, 2):
         g1.second_far(k)
+    acc[...] = jnp.zeros_like(acc)
+    pass_tokens(3)
     g2.second_near(3)
-    pass_tokens(2)
+    siblings(0)
+    for i in (0, 1):
+        need_tokens(i)
+        dots(0, 2 * i, 2 * i + 2)
     g2.second_near(1)
-    pass_tokens(3)
-    siblings(0)
-    need_tokens()
-    dots(0)
+    need_tokens(2)
+    dots(0, 4, 6)
+    g2.second_near(2)
+    siblings(1)
+    dots(1, 0, 6)
+    need_tokens(3)
+    dots(0, 6, 8)
     sums[0, 0] = row_sum(1)
-    g2.second_near(2)
+    dots(1, 6, 8)
 
     partner = (x, s + 1 - 2 * yh, tp)
     z_up, z_down = (x, ((z + 1) % 4) * 2 + yh, tp), (x, ((z + 3) % 4) * 2 + yh, tp)
@@ -443,51 +459,47 @@
         return remote(wo_place(z2, yh2), wo_place(z2, yh2), wo_send.at[i], wo_recv.at[i], device)
 
     z_prev, z_next, z_far = (z + 3) % 4, (z + 1) % 4, (z + 2) % 4
-    relay(3)
-    arrive(3)
-    wo_steps = [wo_copy(0, z, yh, partner), wo_copy(1, z, yh, z_up), wo_copy(2, z, yh, z_down)]
-    for copy in wo_steps:
+    wo_steps = []
+
+    def wo_more(copy):
         copy.start()
-
-    siblings(1)
+        wo_steps.append(copy)
+
     key_shares = share(0)
     for copy in key_shares:
         copy.start()
-
-    def wo_more(copy):
-        copy.start()
-        wo_steps.append(copy)
-
-    wo_copy(0, z, other, partner).wait_recv()
-    wo_more(wo_copy(3, z, other, z_up))
-    wo_more(wo_copy(4, z, other, z_down))
-    dots(1)
     kv_out[:, COLS:] = acc[2].astype(jnp.bfloat16)
-    wo_copy(1, z_prev, yh, partner).wait_recv()
-    wo_more(wo_copy(5, z_prev, yh, z_up))
+    for k in (0, 3, 1, 2):
+        g2.second_far(k)
+    relay(3)
+    arrive(3)
+    wo_more(wo_copy(0, z, yh, partner))
+    wo_more(wo_copy(1, z, yh, z_up))
+    wo_more(wo_copy(2, z, yh, z_down))
     for copy in key_shares:
         copy.wait()
     gains = gain[...].astype(jnp.float32)
     kv_out[:, :COLS] = (acc[1] * scale_of(0) * gains[1:2]).astype(jnp.bfloat16)
-    for k in (0, 3, 1, 2):
-        g2.second_far(k)
-    wo_copy(4, z_next, other, partner).wait_recv()
-    wo_more(wo_copy(6, z_next, other, z_down))
     siblings(2)
-    dots(2)
+    dots(2, 0, 8)
     sums[1, 0] = row_sum(0)
-    wo_copy(2, z_next, yh, partner).wait_recv()
-    wo_copy(3, z_prev, other, partner).wait_recv()
+    wo_copy(0, z, other, partner).wait_recv()
+    wo_more(wo_copy(3, z, other, z_up))
+    wo_more(wo_copy(4, z, other, z_down))
+    wo_copy(1, z_prev, yh, partner).wait_recv()
+    wo_more(wo_copy(5, z_prev, yh, z_up))
     query_shares = share(1)
     for copy in query_shares:
         copy.start()
+    wo_copy(4, z_next, other, partner).wait_recv()
+    wo_more(wo_copy(6, z_next, other, z_down))
+    wo_copy(2, z_next, yh, partner).wait_recv()
+    wo_copy(3, z_prev, other, partner).wait_recv()
     for gather in parts:
         gather.finish()
 
-    @pl.when(x == root)
-    def _():
-        for group in range(4):
-            pl.when(tp == group)(lambda group=group: root_copies(group, drain))
+    at_root(root_copies, drain)
+    at_root(root_wo, drain)
 
     @pl.when(x == mid)
     def _():

time: 231 us -> 228 us (0.987); the launches traced: 230 us -> 230 us
    pallas_call x1, Pallas kernels: 128 us -> 119 us  [qkv_call(): pl.pallas_call(lambda *refs: qkv_kernel(root, *refs), out_shape=[jax.Shap...]
    pallas_call x1, Pallas kernels: 90.6 us -> 99.8 us  [attend_call(): pl.pallas_call(attend_kernel, out_shape=[jax.ShapeDtypeStruct((ROWS, D //...]
where the time goes in v4:
time: 228 us; the launch traced here: 230 us
  Pallas kernels  218 us (96%)
  local copies, waits for them, and re-layouts  8.55 us (4%)
    pallas_call x1, Pallas kernels, qkv_call(): pl.pallas_call(lambda *refs: qkv_kernel(root, *refs), out_shape=[jax.Shap...  119 us
    pallas_call x1, Pallas kernels, attend_call(): pl.pallas_call(attend_kernel, out_shape=[jax.ShapeDtypeStruct((ROWS, D //...  99.8 us

profile of v4, /device:TPU:1, one launch (start us, length us, event | category | flops | bytes accessed | tf_op | source)
XLA Modules:
  0.0 229.7 jit_solution(8281917604794668927)
XLA Ops:
  0.6 0.0 copy-start
  2.0 0.7 dynamic-slice_bitcast_fusion.2
  2.7 0.0 copy-done
  2.7 0.3 fusion
  3.1 1.2 dynamic-slice_bitcast_fusion.1
  4.4 3.4 %dynamic-slice_bitcast_fusion = bf16[3,640,640]{2,1,0:T(8,128)(2,1)} fusion(bf16[4,640,3,640]{3,1,2,0:T(8,128)(2,1)} %param.14, s32[]{:T(128)S(6)} %select_n.21), kind=kLoop, calls=%fused_computation | loop fusion | bytes 4915204 | tf_op jit(solution)/shard_map/jit(dynamic_index_in_dim)/squeeze | solution.py:868
  7.7 118.9 %conditional.1 = ((bf16[256,640]{1,0:T(8,128)(2,1)S(1)}, bf16[256,1280]{1,0:T(8,128)(2,1)}, bf16[640,1280]{1,0:T(8,128)(2,1)})) conditional(s32[]{:T(128)} %clamp.3, (bf16[3,640,640]{2,1,0:T(8,128)(2,1)}, bf16[640,640]{1,0:T(8,128)(2,1)S(1)}, bf16[16,640]{1,0:T(8,128)(2,1)S(1)}, bf16[256,5120]{1,0:T(8,128)(2,1)}, ...), branch_computations={%region_0.1_spmd, %region_1.2_spmd, %region_2.3_spmd, %region_3.4_... | conditional | bytes 8 | solution.py:875
  7.7 118.7 %qkv_3.1 = (bf16[256,640]{1,0:T(8,128)(2,1)S(1)}, bf16[256,1280]{1,0:T(8,128)(2,1)}, bf16[640,1280]{1,0:T(8,128)(2,1)}) custom-call(bf16[3,640,640]{2,1,0:T(8,128)(2,1)} %get-tuple-element.55.refs_0_, bf16[640,640]{1,0:T(8,128)(2,1)S(1)} %get-tuple-element.56.refs_1_, bf16[16,640]{1,0:T(8,128)(2,1)S(1)} %get-tuple-element.57.refs_2_, ...), custom_call_target="tpu_custom_call" | custom-call | tf_op jit(solution)/shard_map/cond/branch_3_fun/qkv_3/pallas_call | solution.py:530
  126.7 99.8 %attend.1 = (bf16[256,1280]{1,0:T(8,128)(2,1)}, f32[8,256]{1,0:T(8,128)}) custom-call(bf16[256,640]{1,0:T(8,128)(2,1)S(1)} %get-tuple-element.67.q_ref, bf16[256,1280]{1,0:T(8,128)(2,1)} %get-tuple-element.68.kv_ref, bf16[640,1280]{1,0:T(8,128)(2,1)} %get-tuple-element.69.wo_ref, bf16[256,5120]{1,0:T(8,128)(2,1)} %bitcast.29, bf16[256,1280]{1,0:T(8,128)(2,1)} %bitcast.30, ...), custom_call_target="tpu_custom_call" | custom-call | tf_op jit(solution)/shard_map/attend/pallas_call | solution.py:825
  226.5 1.3 slice.3
  227.7 2.0 copy.28
  (3 shorter events, 0.0 us)
Async XLA Ops:
  0.6 2.1 copy-start

commit v5 on v4

--- a/solution.py
+++ b/solution.py
@@ -423,12 +423,12 @@
     g1.second_near(3)
     arrive(2)
     g2.begin()
+    at_root(root_wo, start)
     g1.second_near(1)
     g2.first_near(3)
     g2.first_near(1)
     pass_tokens(2)
     g1.second_near(2)
-    at_root(root_wo, start)
     g2.second_near(0)
     g2.first_far()
     for k in (0, 3, 1, 2):

time: 228 us -> 226 us (level); the launches traced: 230 us -> 223 us
  Pallas kernels: 218 us -> 211 us
    pallas_call x1, Pallas kernels: 99.8 us -> 91.6 us  [attend_call(): pl.pallas_call(attend_kernel, out_shape=[jax.ShapeDtypeStruct((ROWS, D //...]
where the time goes in v5:
time: 226 us; the launch traced here: 223 us
  Pallas kernels  211 us (93%)
  local copies, waits for them, and re-layouts  8.55 us (4%)
    pallas_call x1, Pallas kernels, qkv_call(): pl.pallas_call(lambda *refs: qkv_kernel(root, *refs), out_shape=[jax.Shap...  119 us
    pallas_call x1, Pallas kernels, attend_call(): pl.pallas_call(attend_kernel, out_shape=[jax.ShapeDtypeStruct((ROWS, D //...  91.6 us

profile of v5, /device:TPU:1, one launch (start us, length us, event | category | flops | bytes accessed | tf_op | source)
XLA Modules:
  0.0 222.5 jit_solution(3547813759356612858)
XLA Ops:
  0.6 0.0 copy-start
  2.0 0.7 dynamic-slice_bitcast_fusion.2
  2.7 0.0 copy-done
  2.7 0.3 fusion
  3.1 1.2 dynamic-slice_bitcast_fusion.1
  4.4 3.4 %dynamic-slice_bitcast_fusion = bf16[3,640,640]{2,1,0:T(8,128)(2,1)} fusion(bf16[4,640,3,640]{3,1,2,0:T(8,128)(2,1)} %param.14, s32[]{:T(128)S(6)} %select_n.21), kind=kLoop, calls=%fused_computation | loop fusion | bytes 4915204 | tf_op jit(solution)/shard_map/jit(dynamic_index_in_dim)/squeeze | solution.py:868
  7.7 119.9 %conditional.1 = ((bf16[256,640]{1,0:T(8,128)(2,1)S(1)}, bf16[256,1280]{1,0:T(8,128)(2,1)}, bf16[640,1280]{1,0:T(8,128)(2,1)})) conditional(s32[]{:T(128)} %clamp.3, (bf16[3,640,640]{2,1,0:T(8,128)(2,1)}, bf16[640,640]{1,0:T(8,128)(2,1)S(1)}, bf16[16,640]{1,0:T(8,128)(2,1)S(1)}, bf16[256,5120]{1,0:T(8,128)(2,1)}, ...), branch_computations={%region_0.1_spmd, %region_1.2_spmd, %region_2.3_spmd, %region_3.4_... | conditional | bytes 8 | solution.py:875
  7.7 119.4 %qkv_0.1 = (bf16[256,640]{1,0:T(8,128)(2,1)S(1)}, bf16[256,1280]{1,0:T(8,128)(2,1)}, bf16[640,1280]{1,0:T(8,128)(2,1)}) custom-call(bf16[3,640,640]{2,1,0:T(8,128)(2,1)} %get-tuple-element.40.refs_0_, bf16[640,640]{1,0:T(8,128)(2,1)S(1)} %get-tuple-element.41.refs_1_, bf16[16,640]{1,0:T(8,128)(2,1)S(1)} %get-tuple-element.42.refs_2_, ...), custom_call_target="tpu_custom_call" | custom-call | tf_op jit(solution)/shard_map/cond/branch_0_fun/qkv_0/pallas_call | solution.py:530
  127.7 91.6 %attend.1 = (bf16[256,1280]{1,0:T(8,128)(2,1)}, f32[8,256]{1,0:T(8,128)}) custom-call(bf16[256,640]{1,0:T(8,128)(2,1)S(1)} %get-tuple-element.67.q_ref, bf16[256,1280]{1,0:T(8,128)(2,1)} %get-tuple-element.68.kv_ref, bf16[640,1280]{1,0:T(8,128)(2,1)} %get-tuple-element.69.wo_ref, bf16[256,5120]{1,0:T(8,128)(2,1)} %bitcast.29, bf16[256,1280]{1,0:T(8,128)(2,1)} %bitcast.30, ...), custom_call_target="tpu_custom_call" | custom-call | tf_op jit(solution)/shard_map/attend/pallas_call | solution.py:825
  219.3 1.3 slice.3
  220.5 2.0 copy.28
  (3 shorter events, 0.0 us)
Async XLA Ops:
  0.6 2.1 copy-start
